TPU v7x, 32 devices: a whole 2x2x4 slice. The times are simulated.
32 devices in a mesh: ta: 4 (over y, x), gx: 2 (over core), gy: 4 (over z).
Axes of the slice: x: 2, y: 2, z: 4, core: 2. Of those that a mesh axis runs over, the one named last changes fastest.
Arguments:
- velocity: float32 [3, 4, 32, 64, 256], P(None, 'ta', 'gx', 'gy'), may hold values from -6 to 6
- pressure: float32 [4, 32, 64, 256], P('ta', 'gx', 'gy'), may hold values from -6 to 6
- forcing: float32 [3, 4, 32, 64, 256], P(None, 'ta', 'gx', 'gy'), may hold values from -6 to 6
- source: float32 [4, 32, 64, 256], P('ta', 'gx', 'gy'), may hold values from -6 to 6
- viscosity: float32 [3, 32, 64, 256], P(None, 'gx', 'gy'), may hold values from 0.05 to 0.5
Outputs:
- new_velocity: float32 [3, 4, 32, 64, 256], P(None, 'ta', 'gx', 'gy')
- new_pressure: float32 [4, 32, 64, 256], P('ta', 'gx', 'gy')
All inputs are finite; a program needn't handle non-finite values.
Results may differ from a plain program's by a relative error of at most 0.00002.
Values sent between devices are 32-bit elements; how exact they have to be, the bound alone decides.
A program may use at most 64 MiB of HBM per device.

v0:
```python
import functools

import jax
import jax.numpy as jnp
from jax import lax
from jax.experimental import pallas as pl
from jax.experimental.pallas import tpu as pltpu
from jax.sharding import PartitionSpec as P

relax_factor = 1.5
damping = 0.8
MESH = pl.DeviceIdType.MESH


def loop(lo, hi, body):
    def step(i, carry):
        body(i)
        return carry

    if hi > lo:
        lax.fori_loop(lo, hi, step, 0, unroll=hi - lo)


def row_index(f):
    return lax.broadcasted_iota(jnp.int32, f.shape, 0)


def y_next(f, row):
    n = f.shape[0]
    return jnp.where(row_index(f) == n - 1, row, pltpu.roll(f, n - 1, 0))


def y_last(f, row):
    return jnp.where(row_index(f) == 0, row, pltpu.roll(f, 1, 0))


def z_next(f):
    return pltpu.roll(f, f.shape[1] - 1, 1)


def z_last(f):
    return pltpu.roll(f, 1, 1)


def groups_of(lo, hi, size):
    return [(a, min(a + size, hi)) for a in range(lo, hi, size)]


def kernel(
    slabs, nx_parts, ny_parts, groups,
    vel, prs, frc, src, vis, out_v, out_p,
    V, Pr, F, S, Nu, C, W, SC, c1, c2, OV, OP,
    sE, rE, sI, rI, yu_s, yd_s, yu_r, yd_r, Ch, f_s, f_r, Fh, rP,
    c1d_s, c1u_s, c1d_r, c1u_r, c2x_s, c2y_s, c2y_r,
    load_sem, out_sem, send_sem, recv_sem,
):
    _, nx, ny, nz = vel.shape
    parts = (ny - 4) // 4
    ta, gx, gy = lax.axis_index("ta"), lax.axis_index("gx"), lax.axis_index("gy")
    t_next, t_prev = lax.rem(ta + 1, slabs), lax.rem(ta + slabs - 1, slabs)
    has_next, has_prev = ta < slabs - 1, ta > 0
    xu, xd = lax.rem(gx + 1, nx_parts), lax.rem(gx + nx_parts - 1, nx_parts)
    yu, yd = lax.rem(gy + 1, ny_parts), lax.rem(gy + ny_parts - 1, ny_parts)

    loads = [
        pltpu.make_async_copy(vel, V.at[:, pl.ds(1, nx)], load_sem.at[0]),
        pltpu.make_async_copy(vis, Nu.at[:, pl.ds(1, nx)], load_sem.at[1]),
        pltpu.make_async_copy(prs, Pr.at[pl.ds(0, nx)], load_sem.at[2]),
        pltpu.make_async_copy(frc, F, load_sem.at[3]),
        pltpu.make_async_copy(src, S, load_sem.at[4]),
    ]
    for copy in loads:
        copy.start()

    barrier = pltpu.get_barrier_semaphore()
    for axis, index in (("gx", xu), ("gx", xd), ("gy", yu), ("gy", yd)):
        pl.semaphore_signal(barrier, inc=1, device_id={axis: index}, device_id_type=MESH)

    @pl.when(has_next)
    def _():
        pl.semaphore_signal(barrier, inc=1, device_id={"ta": t_next}, device_id_type=MESH)

    @pl.when(has_prev)
    def _():
        pl.semaphore_signal(barrier, inc=1, device_id={"ta": t_prev}, device_id_type=MESH)

    def remote(k, source, target, axis, index):
        return pltpu.make_async_remote_copy(
            src_ref=source, dst_ref=target, send_sem=send_sem.at[k], recv_sem=recv_sem.at[k],
            device_id={axis: index}, device_id_type=MESH,
        )

    vx_up = remote(0, V.at[:, nx], V.at[:, 0], "gx", xu)
    vx_dn = remote(1, V.at[:, 1], V.at[:, nx + 1], "gx", xd)
    px_dn = remote(2, Pr.at[0], Pr.at[nx], "gx", xd)
    nx_up = remote(3, Nu.at[0, nx], Nu.at[0, 0], "gx", xu)
    ry_up = remote(4, yu_s, yu_r, "gy", yu)
    ry_dn = remote(5, yd_s, yd_r, "gy", yd)
    fx_up = remote(6, W.at[0, nx], W.at[0, 0], "gx", xu)
    fy_up = remote(7, f_s, f_r, "gy", yu)
    cx_dn = remote(8, c1.at[1], c1.at[nx + 1], "gx", xd)
    cx_up = remote(9, c1.at[nx], c1.at[0], "gx", xu)
    cy_dn = remote(10, c1d_s, c1d_r, "gy", yd)
    cy_up = remote(11, c1u_s, c1u_r, "gy", yu)
    ex_dn = remote(12, c2x_s, c2.at[nx], "gx", xd)
    ey_dn = remote(13, c2y_s, c2y_r, "gy", yd)
    edge = remote(14, sE, rE, "ta", t_next)
    border = remote(15, yu_r.at[1], rP, "ta", t_next)
    pieces = [
        remote(16 + k, sI.at[pl.ds(a, b - a)], rI.at[pl.ds(a, b - a)], "ta", t_next)
        for k, (a, b) in enumerate(groups)
    ]

    def pack_edges(x):
        for c in range(3):
            sE[c, x, 0:2] = V[c, x + 1, 0:2]
            sE[c, x, 2:4] = V[c, x + 1, ny - 2 : ny]

    def pack_rows(x):
        for c in range(3):
            yu_s[c, x] = V[c, x + 1, ny - 1 : ny]
            yd_s[c, x] = V[c, x + 1, 0:1]
        yu_s[3, x] = Nu[1, x + 1, ny - 1 : ny]
        yd_s[3, x] = Pr[x, 0:1]

    def pack_inner(x):
        for c in range(3):
            for p in range(parts):
                sI[x, p, c] = V[c, x + 1, 2 + 4 * p : 6 + 4 * p]

    loads[0].wait()
    loop(0, nx, pack_edges)
    pl.semaphore_wait(barrier, 4 + has_next.astype(jnp.int32) + has_prev.astype(jnp.int32))

    @pl.when(has_next)
    def _():
        edge.start()

    loads[1].wait()
    loads[2].wait()
    loop(0, nx, pack_rows)
    for copy in (ry_up, ry_dn, vx_up, vx_dn, px_dn, nx_up):
        copy.start()

    loop(0, nx, pack_inner)

    @pl.when(has_next)
    def _():
        for copy in pieces[:2]:
            copy.start()

    ry_up.wait_recv()

    @pl.when(has_next)
    def _():
        for copy in (border, *pieces[2:]):
            copy.start()

    def coeff_of(nu):
        return 1.0 / (relax_factor * (1.0 + 6.0 * nu))

    loads[3].wait()
    loads[4].wait()
    for copy in (vx_up, vx_dn, px_dn, nx_up, ry_dn):
        copy.wait_recv()
    C[0, 0] = coeff_of(Nu[0, 0])

    def prepare(x):
        e = x + 1
        below = coeff_of(yu_r[3, x])
        Ch[x] = below
        coeff = [coeff_of(Nu[c, e]) for c in range(3)]
        for c in range(3):
            C[c, e] = coeff[c]
        total = coeff[0] + C[0, x] + coeff[1] + y_last(coeff[1], below) + coeff[2] + z_last(coeff[2])
        SC[x] = damping / total
        press = Pr[x]
        grads = (Pr[x + 1] - press, y_next(press, yd_r[3, x]) - press, z_next(press) - press)
        for c in range(3):
            v = V[c, e]
            near = V[c, e - 1] + V[c, e + 1] + y_last(v, yu_r[c, x]) + y_next(v, yd_r[c, x])
            near = near + z_last(v) + z_next(v)
            momentum = F[c, x] - (v + Nu[c, e] * (6.0 * v - near)) - grads[c]
            W[c, e] = v + coeff[c] * momentum
        f_s[x] = W[1, e, ny - 1 : ny]

    loop(0, nx, prepare)
    fy_up.start()

    def add_edges(x):
        for c in range(3):
            for s, t in ((0, 0), (2, ny - 2)):
                W[c, x + 1, t : t + 2] = (
                    W[c, x + 1, t : t + 2] + C[c, x + 1, t : t + 2] * rE[c, x, s : s + 2]
                )

    def add_inner(x):
        for c in range(3):
            for p in range(parts):
                t = 2 + 4 * p
                W[c, x + 1, t : t + 4] = W[c, x + 1, t : t + 4] + C[c, x + 1, t : t + 4] * rI[x, p, c]

    def arrive(k):
        @pl.when(has_prev)
        def _():
            pieces[k].wait_recv()
            loop(*groups[k], add_inner)

    @pl.when(has_prev)
    def _():
        edge.wait_recv()
        loop(0, nx, add_edges)

    arrive(0)
    arrive(1)
    fx_up.start()
    fy_up.wait_recv()

    @pl.when(has_prev)
    def _():
        border.wait_recv()
        Fh[...] = f_r[...] + Ch[...] * rP[...]

    @pl.when(jnp.logical_not(has_prev))
    def _():
        Fh[...] = f_r[...]

    fx_up.wait_recv()

    def sweep_one(x):
        e = x + 1
        w1, w2 = W[1, e], W[2, e]
        div = (W[0, e] - W[0, x]) + (w1 - y_last(w1, Fh[x])) + (w2 - z_last(w2))
        return SC[x] * (S[x] - div)

    def first_edges(x):
        change = sweep_one(x)
        c1[x + 1] = change
        c1d_s[x] = change[0:1]
        c1u_s[x] = change[ny - 1 : ny]

    loop(0, nx, first_edges)
    for copy in (cy_dn, cy_up, cx_dn, cx_up):
        copy.start()
    for copy in (cx_dn, cx_up, cy_dn, cy_up):
        copy.wait_recv()

    def sweep_two(x):
        e = x + 1
        here = c1[e]
        w0 = W[0, e] - C[0, e] * (c1[e + 1] - here)
        w0_last = W[0, x] - C[0, x] * (here - c1[x])
        w1 = W[1, e] - C[1, e] * (y_next(here, c1d_r[x]) - here)
        row = Fh[x] - Ch[x] * (here[0:1] - c1u_r[x])
        w2 = W[2, e] - C[2, e] * (z_next(here) - here)
        div = (w0 - w0_last) + (w1 - y_last(w1, row)) + (w2 - z_last(w2))
        return here + SC[x] * (S[x] - div)

    c2x_s[...] = sweep_two(0)

    def second_edges(x):
        c2y_s[x] = sweep_two(x)[0:1]

    loop(0, nx, second_edges)
    ey_dn.start()
    ex_dn.start()

    for copy in (cx_dn, cx_up):
        copy.wait_send()

    def first(x):
        c1[x + 1] = sweep_one(x)

    def second(x):
        c2[x] = sweep_two(x)

    def finish(x):
        e = x + 1
        here = c2[x]
        OP[x] = Pr[x] + here
        OV[0, x] = W[0, e] - C[0, e] * (c2[x + 1] - here)
        OV[1, x] = W[1, e] - C[1, e] * (y_next(here, c2y_r[x]) - here)
        OV[2, x] = W[2, e] - C[2, e] * (z_next(here) - here)

    stores = []

    def emit(a, b):
        k = len(stores)
        loop(a, b, finish)
        part = pl.ds(a, b - a)
        stores.append(pltpu.make_async_copy(OV.at[:, part], out_v.at[:, part], out_sem.at[k]))
        stores.append(pltpu.make_async_copy(OP.at[part], out_p.at[part], out_sem.at[k + 1]))
        for copy in stores[-2:]:
            copy.start()

    done = 0
    for k in range(2, len(groups)):
        last = k == len(groups) - 1
        if last:
            ex_dn.wait_recv()
            ey_dn.wait_recv()
            ready = done - 2
            emit(0, ready)
        arrive(k)
        stop = nx if last else groups[k][1]
        loop(done, stop, first)
        loop(max(done - 1, 0), nx if last else stop - 1, second)
        done = stop
    emit(ready, nx)

    @pl.when(has_next)
    def _():
        edge.wait_send()
        border.wait_send()
        for copy in pieces:
            copy.wait_send()

    for copy in (vx_up, vx_dn, px_dn, nx_up, ry_up, ry_dn, fx_up, fy_up, cy_dn, cy_up, ex_dn, ey_dn):
        copy.wait_send()
    for copy in stores:
        copy.wait()


def place(from_v, from_p, out_v, out_p, sem):
    copies = [
        pltpu.make_async_copy(from_v.at[c], out_v.at[c], sem.at[c]) for c in range(3)
    ] + [pltpu.make_async_copy(from_p, out_p, sem.at[3])]
    for copy in copies:
        copy.start()
    for copy in copies:
        copy.wait()


def body(counts, velocity, pressure, forcing, source, viscosity):
    _, steps, nx, ny, nz = velocity.shape
    assert steps == 1 and nx >= 8 and ny >= 8 and ny % 4 == 0
    groups = [(0, 2), (nx - 2, nx)] + groups_of(2, nx - 4, 5) + [(nx - 4, nx - 2)]
    parts = (ny - 4) // 4
    vmem = lambda *shape: pltpu.VMEM(shape, jnp.float32)
    rows = lambda *lead: vmem(*lead, nx, 1, nz)
    any_space = pl.BlockSpec(memory_space=pl.ANY)
    out_v, out_p = pl.pallas_call(
        functools.partial(kernel, *counts, groups),
        out_shape=(
            jax.ShapeDtypeStruct((3, nx, ny, nz), jnp.float32),
            jax.ShapeDtypeStruct((nx, ny, nz), jnp.float32),
        ),
        in_specs=[any_space] * 5,
        out_specs=(any_space, any_space),
        scratch_shapes=[
            vmem(3, nx + 2, ny, nz), vmem(nx + 1, ny, nz), vmem(3, nx, ny, nz), vmem(nx, ny, nz),
            vmem(3, nx + 1, ny, nz), vmem(3, nx + 1, ny, nz), vmem(3, nx + 1, ny, nz),
            vmem(nx, ny, nz), vmem(nx + 2, ny, nz), vmem(nx + 1, ny, nz),
            vmem(3, nx, ny, nz), vmem(nx, ny, nz),
            vmem(3, nx, 4, nz), vmem(3, nx, 4, nz),
            vmem(nx, parts, 3, 4, nz), vmem(nx, parts, 3, 4, nz),
            rows(4), rows(4), rows(4), rows(4), rows(), rows(), rows(), rows(), rows(),
            rows(), rows(), rows(), rows(), vmem(ny, nz), rows(), rows(),
            pltpu.SemaphoreType.DMA((5,)),
            pltpu.SemaphoreType.DMA((4,)),
            pltpu.SemaphoreType.DMA((16 + len(groups),)),
            pltpu.SemaphoreType.DMA((16 + len(groups),)),
        ],
        compiler_params=pltpu.CompilerParams(
            collective_id=0, has_side_effects=True, vmem_limit_bytes=48 << 20
        ),
        name="smoother",
    )(*(pltpu.with_memory_space_constraint(a, pltpu.HBM) for a in (velocity[:, 0], pressure[0], forcing[:, 0], source[0], viscosity)))
    out_v, out_p = pl.pallas_call(
        place,
        out_shape=(
            jax.ShapeDtypeStruct(out_v.shape, jnp.float32),
            jax.ShapeDtypeStruct(out_p.shape, jnp.float32),
        ),
        in_specs=[any_space] * 2,
        out_specs=(any_space, any_space),
        scratch_shapes=[pltpu.SemaphoreType.DMA((4,))],
        compiler_params=pltpu.CompilerParams(vmem_limit_bytes=1 << 20),
        name="place",
    )(out_v, out_p)
    return out_v[:, None], out_p[None]


def solution(mesh):
    placed = (
        P(None, "ta", "gx", "gy", None),
        P("ta", "gx", "gy", None),
        P(None, "ta", "gx", "gy", None),
        P("ta", "gx", "gy", None),
        P(None, "gx", "gy", None),
    )
    counts = tuple(mesh.shape[axis] for axis in ("ta", "gx", "gy"))
    return jax.shard_map(
        functools.partial(body, counts),
        mesh=mesh,
        in_specs=placed,
        out_specs=(P(None, "ta", "gx", "gy", None), P("ta", "gx", "gy", None)),
        check_vma=False,
    )
```

profile of v0, /device:TPU:4, one launch (start us, length us, event | category | flops | bytes accessed | tf_op | source)
XLA Modules:
  0.0 25.4 jit_solution(11566982304664729879)
XLA Ops:
  0.6 23.7 %smoother.1 = (f32[3,16,16,256]{3,2,1,0:T(8,128)S(1)}, f32[16,16,256]{2,1,0:T(8,128)S(1)}) custom-call(f32[3,16,16,256]{3,2,1,0:T(8,128)} %bitcast.8, f32[16,16,256]{2,1,0:T(8,128)} %bitcast.10, f32[3,16,16,256]{3,2,1,0:T(8,128)} %bitcast.9, f32[16,16,256]{2,1,0:T(8,128)} %bitcast.11, f32[3,16,16,256]{3,2,1,0:T(8,128)} %vis.1), custom_call_target="tpu_custom_call" | custom-call | tf_op jit(solution)/shard_map/smoother/pallas_call | solution.py:342
  24.4 1.0 %place.1 = (f32[3,16,16,256]{3,2,1,0:T(8,128)}, f32[16,16,256]{2,1,0:T(8,128)}) custom-call(f32[3,16,16,256]{3,2,1,0:T(8,128)S(1)} %get-tuple-element.6.from_v, f32[16,16,256]{2,1,0:T(8,128)S(1)} %get-tuple-element.7.from_p), custom_call_target="tpu_custom_call" | custom-call | tf_op jit(solution)/shard_map/place/pallas_call | solution.py:369
where the time goes:
time: 25.5 us; the launch traced here: 25.4 us
  Pallas kernels  24.7 us (97%)
  between operations  0.64 us (3%)
    pallas_call x1, Pallas kernels, body(): pl.pallas_call(functools.partial(kernel, *counts, groups), out_shape=(jax...  23.7 us
    pallas_call x1, Pallas kernels, body(): pl.pallas_call(place, out_shape=(jax.ShapeDtypeStruct(out_v.shape, jnp.fl...  1 us

commit v1 on v0

--- a/solution.py
+++ b/solution.py
@@ -50,7 +50,7 @@
     slabs, nx_parts, ny_parts, groups,
     vel, prs, frc, src, vis, out_v, out_p,
     V, Pr, F, S, Nu, C, W, SC, c1, c2, OV, OP,
-    sE, rE, sI, rI, yu_s, yd_s, yu_r, yd_r, Ch, f_s, f_r, Fh, rP,
+    sE, rE, sI, rI, yu_s, yd_s, yu_r, yd_r, Ch, f_s, Fh,
     c1d_s, c1u_s, c1d_r, c1u_r, c2x_s, c2y_s, c2y_r,
     load_sem, out_sem, send_sem, recv_sem,
 ):
@@ -73,16 +73,23 @@
         copy.start()
 
     barrier = pltpu.get_barrier_semaphore()
-    for axis, index in (("gx", xu), ("gx", xd), ("gy", yu), ("gy", yd)):
+
+    def greet(axis, index):
         pl.semaphore_signal(barrier, inc=1, device_id={axis: index}, device_id_type=MESH)
 
-    @pl.when(has_next)
-    def _():
-        pl.semaphore_signal(barrier, inc=1, device_id={"ta": t_next}, device_id_type=MESH)
+    first_row = gy == 0
+    greet("gx", xu)
+    greet("gx", xd)
 
     @pl.when(has_prev)
     def _():
-        pl.semaphore_signal(barrier, inc=1, device_id={"ta": t_prev}, device_id_type=MESH)
+        greet("ta", t_prev)
+
+    for beside in (yu, yd):
+
+        @pl.when(jnp.logical_not(first_row) & (beside != 0))
+        def _():
+            greet("gy", beside)
 
     def remote(k, source, target, axis, index):
         return pltpu.make_async_remote_copy(
@@ -97,7 +104,7 @@
     ry_up = remote(4, yu_s, yu_r, "gy", yu)
     ry_dn = remote(5, yd_s, yd_r, "gy", yd)
     fx_up = remote(6, W.at[0, nx], W.at[0, 0], "gx", xu)
-    fy_up = remote(7, f_s, f_r, "gy", yu)
+    fy_up = remote(7, f_s, Fh, "gy", yu)
     cx_dn = remote(8, c1.at[1], c1.at[nx + 1], "gx", xd)
     cx_up = remote(9, c1.at[nx], c1.at[0], "gx", xu)
     cy_dn = remote(10, c1d_s, c1d_r, "gy", yd)
@@ -105,9 +112,8 @@
     ex_dn = remote(12, c2x_s, c2.at[nx], "gx", xd)
     ey_dn = remote(13, c2y_s, c2y_r, "gy", yd)
     edge = remote(14, sE, rE, "ta", t_next)
-    border = remote(15, yu_r.at[1], rP, "ta", t_next)
     pieces = [
-        remote(16 + k, sI.at[pl.ds(a, b - a)], rI.at[pl.ds(a, b - a)], "ta", t_next)
+        remote(15 + k, sI.at[pl.ds(a, b - a)], rI.at[pl.ds(a, b - a)], "ta", t_next)
         for k, (a, b) in enumerate(groups)
     ]
 
@@ -130,7 +136,12 @@
 
     loads[0].wait()
     loop(0, nx, pack_edges)
-    pl.semaphore_wait(barrier, 4 + has_next.astype(jnp.int32) + has_prev.astype(jnp.int32))
+    pl.semaphore_wait(barrier, 2 + has_next.astype(jnp.int32) + jnp.where(first_row, 0, 2))
+    for beside in (yu, yd):
+
+        @pl.when(first_row | (beside == 0))
+        def _():
+            greet("gy", beside)
 
     @pl.when(has_next)
     def _():
@@ -139,29 +150,33 @@
     loads[1].wait()
     loads[2].wait()
     loop(0, nx, pack_rows)
-    for copy in (ry_up, ry_dn, vx_up, vx_dn, px_dn, nx_up):
+    for copy in (vx_up, vx_dn, px_dn, nx_up):
         copy.start()
 
+    @pl.when(jnp.logical_not(first_row))
+    def _():
+        ry_up.start()
+        ry_dn.start()
+
     loop(0, nx, pack_inner)
 
     @pl.when(has_next)
     def _():
-        for copy in pieces[:2]:
+        for copy in pieces:
             copy.start()
 
-    ry_up.wait_recv()
-
-    @pl.when(has_next)
-    def _():
-        for copy in (border, *pieces[2:]):
-            copy.start()
+    @pl.when(first_row)
+    def _():
+        pl.semaphore_wait(barrier, 2)
+        ry_up.start()
+        ry_dn.start()
 
     def coeff_of(nu):
         return 1.0 / (relax_factor * (1.0 + 6.0 * nu))
 
     loads[3].wait()
     loads[4].wait()
-    for copy in (vx_up, vx_dn, px_dn, nx_up, ry_dn):
+    for copy in (vx_up, vx_dn, px_dn, nx_up, ry_up, ry_dn):
         copy.wait_recv()
     C[0, 0] = coeff_of(Nu[0, 0])
 
@@ -182,10 +197,8 @@
             near = near + z_last(v) + z_next(v)
             momentum = F[c, x] - (v + Nu[c, e] * (6.0 * v - near)) - grads[c]
             W[c, e] = v + coeff[c] * momentum
-        f_s[x] = W[1, e, ny - 1 : ny]
 
     loop(0, nx, prepare)
-    fy_up.start()
 
     def add_edges(x):
         for c in range(3):
@@ -211,19 +224,15 @@
         edge.wait_recv()
         loop(0, nx, add_edges)
 
+    def pack_flux(x):
+        f_s[x] = W[1, x + 1, ny - 1 : ny]
+
+    loop(0, nx, pack_flux)
+    fy_up.start()
     arrive(0)
     arrive(1)
     fx_up.start()
     fy_up.wait_recv()
-
-    @pl.when(has_prev)
-    def _():
-        border.wait_recv()
-        Fh[...] = f_r[...] + Ch[...] * rP[...]
-
-    @pl.when(jnp.logical_not(has_prev))
-    def _():
-        Fh[...] = f_r[...]
 
     fx_up.wait_recv()
 
@@ -311,7 +320,6 @@
     @pl.when(has_next)
     def _():
         edge.wait_send()
-        border.wait_send()
         for copy in pieces:
             copy.wait_send()
 
@@ -354,12 +362,12 @@
             vmem(3, nx, ny, nz), vmem(nx, ny, nz),
             vmem(3, nx, 4, nz), vmem(3, nx, 4, nz),
             vmem(nx, parts, 3, 4, nz), vmem(nx, parts, 3, 4, nz),
-            rows(4), rows(4), rows(4), rows(4), rows(), rows(), rows(), rows(), rows(),
+            rows(4), rows(4), rows(4), rows(4), rows(), rows(), rows(),
             rows(), rows(), rows(), rows(), vmem(ny, nz), rows(), rows(),
             pltpu.SemaphoreType.DMA((5,)),
             pltpu.SemaphoreType.DMA((4,)),
-            pltpu.SemaphoreType.DMA((16 + len(groups),)),
-            pltpu.SemaphoreType.DMA((16 + len(groups),)),
+            pltpu.SemaphoreType.DMA((15 + len(groups),)),
+            pltpu.SemaphoreType.DMA((15 + len(groups),)),
         ],
         compiler_params=pltpu.CompilerParams(
             collective_id=0, has_side_effects=True, vmem_limit_bytes=48 << 20

time: 25.5 us -> 25.6 us (level)
  the two profiles are of different devices: /device:TPU:4 before, /device:TPU:0 now
where the time goes in v1:
time: 25.6 us; the launch traced here: 25.4 us
  Pallas kernels  24.8 us (97%)
  between operations  0.64 us (2%)
    pallas_call x1, Pallas kernels, body(): pl.pallas_call(functools.partial(kernel, *counts, groups), out_shape=(jax...  23.8 us
    pallas_call x1, Pallas kernels, body(): pl.pallas_call(place, out_shape=(jax.ShapeDtypeStruct(out_v.shape, jnp.fl...  1 us

profile of v1, /device:TPU:0, one launch (start us, length us, event | category | flops | bytes accessed | tf_op | source)
XLA Modules:
  0.0 25.4 jit_solution(18368734185602562066)
XLA Ops:
  0.6 23.8 %smoother.1 = (f32[3,16,16,256]{3,2,1,0:T(8,128)S(1)}, f32[16,16,256]{2,1,0:T(8,128)S(1)}) custom-call(f32[3,16,16,256]{3,2,1,0:T(8,128)} %bitcast.8, f32[16,16,256]{2,1,0:T(8,128)} %bitcast.10, f32[3,16,16,256]{3,2,1,0:T(8,128)} %bitcast.9, f32[16,16,256]{2,1,0:T(8,128)} %bitcast.11, f32[3,16,16,256]{3,2,1,0:T(8,128)} %vis.1), custom_call_target="tpu_custom_call" | custom-call | tf_op jit(solution)/shard_map/smoother/pallas_call | solution.py:350
  24.4 1.0 %place.1 = (f32[3,16,16,256]{3,2,1,0:T(8,128)}, f32[16,16,256]{2,1,0:T(8,128)}) custom-call(f32[3,16,16,256]{3,2,1,0:T(8,128)S(1)} %get-tuple-element.6.from_v, f32[16,16,256]{2,1,0:T(8,128)S(1)} %get-tuple-element.7.from_p), custom_call_target="tpu_custom_call" | custom-call | tf_op jit(solution)/shard_map/place/pallas_call | solution.py:377

commit v2 on v1

v2 whole, which is shorter than its diff:
```python
import functools

import jax
import jax.numpy as jnp
from jax import lax
from jax.experimental import pallas as pl
from jax.experimental.pallas import tpu as pltpu
from jax.sharding import PartitionSpec as P

relax_factor = 1.5
damping = 0.8
MESH = pl.DeviceIdType.MESH


def loop(lo, hi, body):
    def step(i, carry):
        body(i)
        return carry

    if hi > lo:
        lax.fori_loop(lo, hi, step, 0, unroll=hi - lo)


def row_index(f):
    return lax.broadcasted_iota(jnp.int32, f.shape, 0)


def y_next(f, row):
    n = f.shape[0]
    return jnp.where(row_index(f) == n - 1, row, pltpu.roll(f, n - 1, 0))


def y_last(f, row):
    return jnp.where(row_index(f) == 0, row, pltpu.roll(f, 1, 0))


def z_next(f):
    return pltpu.roll(f, f.shape[1] - 1, 1)


def z_last(f):
    return pltpu.roll(f, 1, 1)


def coeff_of(nu):
    return 1.0 / (relax_factor * (1.0 + 6.0 * nu))


def groups_of(lo, hi, size):
    return [(a, min(a + size, hi)) for a in range(lo, hi, size)]


def first_change(scale, source, w0, w0_last, w1, row, w2):
    div = (w0 - w0_last) + (w1 - y_last(w1, row)) + (w2 - z_last(w2))
    return scale * (source - div)


def second_change(scale, here, x_above, x_below, above, row, c0, c0_last, c1, c1_row, c2):
    g0, g0_last = c0 * (x_above - here), c0_last * (here - x_below)
    g1 = c1 * (y_next(here, above) - here)
    g2 = c2 * (z_next(here) - here)
    div = (g0 - g0_last) + (g1 - y_last(g1, c1_row * (here[0:1] - row))) + (g2 - z_last(g2))
    return 2.0 * here + scale * div


def final_velocity(w, c, here, x_above, above):
    return (
        w[0] - c[0] * (x_above - here),
        w[1] - c[1] * (y_next(here, above) - here),
        w[2] - c[2] * (z_next(here) - here),
    )


def kernel(
    slabs, nx_parts, ny_parts, groups, detour,
    vel, prs, frc, src, vis,
    OV, OP, rL, W, C, c1, c2, c2e, SC, S, Pr, up_r, Ch,
    V, F, Nu, sE, rE, sI, rI, rR, yu_s, yd_s, yu_r, yd_r, Ce, m_s, fe_s, fe_r, up_s, dn_s, dn_r,
    load_sem, send_sem, recv_sem,
):
    _, nx, ny, nz = vel.shape
    parts = (ny - 4) // 4
    final = len(groups) - 1
    ta, gx, gy = lax.axis_index("ta"), lax.axis_index("gx"), lax.axis_index("gy")
    t_next, t_prev = lax.rem(ta + 1, slabs), lax.rem(ta + slabs - 1, slabs)
    has_next, has_prev = ta < slabs - 1, ta > 0
    xu, xd = lax.rem(gx + 1, nx_parts), lax.rem(gx + nx_parts - 1, nx_parts)
    yu, yd = lax.rem(gy + 1, ny_parts), lax.rem(gy + ny_parts - 1, ny_parts)
    first_row = gy == 0

    loads = [
        pltpu.make_async_copy(vel, V.at[:, pl.ds(1, nx)], load_sem.at[0]),
        pltpu.make_async_copy(vis, Nu.at[:, pl.ds(1, nx)], load_sem.at[1]),
        pltpu.make_async_copy(prs, Pr.at[pl.ds(0, nx)], load_sem.at[2]),
        pltpu.make_async_copy(frc, F, load_sem.at[3]),
        pltpu.make_async_copy(src, S, load_sem.at[4]),
    ]
    for copy in loads:
        copy.start()

    barrier = pltpu.get_barrier_semaphore()

    def greet(axis, index):
        pl.semaphore_signal(barrier, inc=1, device_id={axis: index}, device_id_type=MESH)

    greet("gx", xu)
    greet("gx", xd)

    @pl.when(has_prev)
    def _():
        greet("ta", t_prev)

    expected = 2 + has_next.astype(jnp.int32) + jnp.where(first_row, 0, 2)
    if detour:
        giver, via, taker, lane = detour

        @pl.when(ta == via)
        def _():
            greet("ta", giver)

        @pl.when(ta == taker)
        def _():
            greet("ta", via)

        expected = expected + ((ta == giver) | (ta == via)).astype(jnp.int32)

    for beside in (yu, yd):

        @pl.when(jnp.logical_not(first_row) & (beside != 0))
        def _():
            greet("gy", beside)

    def remote(k, source, target, axis, index):
        return pltpu.make_async_remote_copy(
            src_ref=source, dst_ref=target, send_sem=send_sem.at[k], recv_sem=recv_sem.at[k],
            device_id={axis: index}, device_id_type=MESH,
        )

    vx_up = remote(0, V.at[:, nx], V.at[:, 0], "gx", xu)
    vx_dn = remote(1, V.at[:, 1], V.at[:, nx + 1], "gx", xd)
    px_dn = remote(2, Pr.at[0], Pr.at[nx], "gx", xd)
    nx_up = remote(3, Nu.at[0, nx], Nu.at[0, 0], "gx", xu)
    ry_up = remote(4, yu_s, yu_r, "gy", yu)
    ry_dn = remote(5, yd_s, yd_r, "gy", yd)
    fe_up = remote(6, fe_s, fe_r, "gx", xu)
    fx_up = remote(7, W.at[0, nx], W.at[0, 0], "gx", xu)
    cx_dn = remote(8, c1.at[1], c1.at[nx + 1], "gx", xd)
    cx_up = remote(9, c1.at[nx], c1.at[0], "gx", xu)
    m_dn = remote(10, m_s, Ce.at[:, pl.ds(1, nx)], "gy", yd)
    ce_up = remote(11, Ce.at[0, nx], Ce.at[0, 0], "gx", xu)
    y_up = remote(12, up_s, up_r, "gy", yu)
    y_dn = remote(13, dn_s, dn_r, "gy", yd)
    ex_dn = remote(14, c2.at[0], c2.at[nx], "gx", xd)
    edge = remote(15, sE, rE, "ta", t_next)
    landing = [rI.at[pl.ds(a, b - a)] for a, b in groups[:final]] + [rL]
    leaving = [sI.at[pl.ds(a, b - a)] for a, b in groups]
    pieces = [remote(16 + k, leaving[k], landing[k], "ta", t_next) for k in range(final + 1)]
    if detour:
        to_via = remote(17 + final, leaving[lane], rR, "ta", via)
        from_via = remote(16 + lane, rR, landing[lane], "ta", taker)

    def pack_edges(x):
        for c in range(3):
            sE[c, x, 0:2] = V[c, x + 1, 0:2]
            sE[c, x, 2:4] = V[c, x + 1, ny - 2 : ny]

    def pack_rows(x):
        for c in range(3):
            yu_s[c, x] = V[c, x + 1, ny - 1 : ny]
            yd_s[c, x] = V[c, x + 1, 0:1]
        yu_s[3, x] = Nu[1, x + 1, ny - 1 : ny]
        yd_s[3, x] = Pr[x, 0:1]

    def pack_inner(x):
        for c in range(3):
            for p in range(parts):
                sI[x, p, c] = V[c, x + 1, 2 + 4 * p : 6 + 4 * p]

    loads[0].wait()
    loop(0, nx, pack_edges)
    pl.semaphore_wait(barrier, expected)
    for beside in (yu, yd):

        @pl.when(first_row | (beside == 0))
        def _():
            greet("gy", beside)

    @pl.when(has_next)
    def _():
        edge.start()

    loads[1].wait()
    loads[2].wait()
    loop(0, nx, pack_rows)
    for copy in (vx_up, vx_dn, px_dn, nx_up):
        copy.start()

    @pl.when(jnp.logical_not(first_row))
    def _():
        ry_up.start()
        ry_dn.start()

    loop(0, nx, pack_inner)

    @pl.when(has_next)
    def _():
        for k, copy in enumerate(pieces):
            if detour and k == lane:

                @pl.when(ta == giver)
                def _():
                    to_via.start()

                @pl.when(ta != giver)
                def _():
                    copy.start()

            else:
                copy.start()

    @pl.when(first_row)
    def _():
        pl.semaphore_wait(barrier, 2)
        ry_up.start()
        ry_dn.start()

    loads[3].wait()
    loads[4].wait()
    for copy in (vx_up, vx_dn, px_dn, nx_up, ry_up, ry_dn):
        copy.wait_recv()
    C[0, 0] = coeff_of(Nu[0, 0])

    def prepare(x):
        e = x + 1
        below = coeff_of(yu_r[3, x])
        Ch[x] = below
        coeff = [coeff_of(Nu[c, e]) for c in range(3)]
        for c in range(3):
            C[c, e] = coeff[c]
            m_s[c, x] = coeff[c][0:1]
        total = coeff[0] + C[0, x] + coeff[1] + y_last(coeff[1], below) + coeff[2] + z_last(coeff[2])
        scale = damping / total
        SC[x] = scale
        m_s[3, x] = scale[0:1]
        press = Pr[x]
        grads = (Pr[x + 1] - press, y_next(press, yd_r[3, x]) - press, z_next(press) - press)
        for c in range(3):
            v = V[c, e]
            near = V[c, e - 1] + V[c, e + 1] + y_last(v, yu_r[c, x]) + y_next(v, yd_r[c, x])
            near = near + z_last(v) + z_next(v)
            momentum = F[c, x] - (v + Nu[c, e] * (6.0 * v - near)) - grads[c]
            W[c, e] = v + coeff[c] * momentum

    loop(0, nx, prepare)
    m_dn.start()
    if detour:

        @pl.when(ta == via)
        def _():
            to_via.wait_recv()
            from_via.start()

    def add_edges(x):
        for c in range(3):
            for s, t in ((0, 0), (2, ny - 2)):
                W[c, x + 1, t : t + 2] = (
                    W[c, x + 1, t : t + 2] + C[c, x + 1, t : t + 2] * rE[c, x, s : s + 2]
                )

    def add_inner(x):
        for c in range(3):
            for p in range(parts):
                t = 2 + 4 * p
                W[c, x + 1, t : t + 4] = W[c, x + 1, t : t + 4] + C[c, x + 1, t : t + 4] * rI[x, p, c]

    def arrive(k):
        @pl.when(has_prev)
        def _():
            pieces[k].wait_recv()
            loop(*groups[k], add_inner)

    @pl.when(has_prev)
    def _():
        edge.wait_recv()
        loop(0, nx, add_edges)

    fe_s[...] = W[0, nx]
    fe_up.start()
    fe_up.wait_recv()

    def edge_rows(x, w0_last):
        e = x + 1
        zero = jnp.zeros((1, nz), jnp.float32)
        change = first_change(SC[x], S[x], W[0, e], w0_last, W[1, e], zero, W[2, e])
        up_s[0, x] = W[1, e, ny - 1 : ny]
        up_s[1, x] = change[ny - 1 : ny]
        dn_s[0, x] = change[0:1]
        dn_s[1, x] = change[1:2]

    edge_rows(0, fe_r[...])
    loop(1, nx, lambda x: edge_rows(x, W[0, x]))
    y_up.start()
    y_dn.start()

    arrive(0)
    arrive(1)
    fx_up.start()
    m_dn.wait_recv()
    ce_up.start()
    for copy in (fx_up, y_up, y_dn):
        copy.wait_recv()

    def first(x):
        e = x + 1
        c1[e, 0:ny] = first_change(SC[x], S[x], W[0, e], W[0, x], W[1, e], up_r[0, x], W[2, e])

    def first_above(x):
        e = x + 1
        c1[e, ny : ny + 1] = dn_r[0, x] + Ce[3, e] * W[1, e, ny - 1 : ny]

    loop(0, nx, first)
    loop(0, nx, first_above)
    for copy in (cx_dn, cx_up):
        copy.start()
    for copy in (cx_dn, cx_up, ce_up):
        copy.wait_recv()

    def second(x):
        e = x + 1
        c2[x] = second_change(
            SC[x], c1[e, 0:ny], c1[e + 1, 0:ny], c1[e - 1, 0:ny], c1[e, ny : ny + 1], up_r[1, x],
            C[0, e], C[0, x], C[1, e], Ch[x], C[2, e],
        )

    def second_above(x):
        e = x + 1
        wide = lambda row: jnp.broadcast_to(row, (8, nz))
        here = wide(c1[e, ny : ny + 1])
        g0 = wide(Ce[0, e]) * (wide(c1[e + 1, ny : ny + 1]) - here)
        g0_last = wide(Ce[0, x]) * (here - wide(c1[e - 1, ny : ny + 1]))
        g1 = wide(Ce[1, e]) * (wide(dn_r[1, x]) - here)
        g1_last = wide(C[1, e, ny - 1 : ny]) * (here - wide(c1[e, ny - 1 : ny]))
        g2 = wide(Ce[2, e]) * (z_next(here) - here)
        div = (g0 - g0_last) + (g1 - g1_last) + (g2 - z_last(g2))
        c2e[x] = (2.0 * here + wide(Ce[3, e]) * div)[0:1]

    second(0)
    ex_dn.start()
    loop(0, nx, second_above)

    def finish(x):
        e = x + 1
        here = c2[x]
        OP[x] = Pr[x] + here
        moved = final_velocity(
            [W[c, e] for c in range(3)], [C[c, e] for c in range(3)], here, c2[x + 1], c2e[x]
        )
        for c in range(3):
            OV[c, x] = moved[c]

    for k in range(2, final):
        a, b = groups[k]
        arrive(k)
        loop(a, b, first)
        loop(a - 1, b - 1, second)
        loop(a - 2, b - 2, finish)

    ex_dn.wait_recv()

    @pl.when(has_prev)
    def _():
        pieces[final].wait_recv()

    @pl.when(jnp.logical_not(has_prev))
    def _():
        rL[...] = jnp.zeros_like(rL)

    @pl.when(has_next)
    def _():
        edge.wait_send()
        for k, copy in enumerate(pieces):
            if detour and k == lane:

                @pl.when(ta == giver)
                def _():
                    to_via.wait_send()

                @pl.when(ta != giver)
                def _():
                    copy.wait_send()

            else:
                copy.wait_send()

    if detour:

        @pl.when(ta == via)
        def _():
            from_via.wait_send()

    for copy in (
        vx_up, vx_dn, px_dn, nx_up, ry_up, ry_dn, fe_up, fx_up, cx_dn, cx_up, m_dn, ce_up, y_up, y_dn, ex_dn
    ):
        copy.wait_send()


def settle(
    last, moved, pressed, rL, W, C, c1, c2, c2e, SC, S, Pr, up_r, Ch, out_v, out_p, nV, nP, nW, n1, n2, sem
):
    _, nx, ny, nz = out_v.shape
    parts = (ny - 4) // 4
    a, b = last
    ready = a - 2

    early = [
        pltpu.make_async_copy(moved.at[c, pl.ds(0, ready)], out_v.at[c, pl.ds(0, ready)], sem.at[c])
        for c in range(3)
    ] + [pltpu.make_async_copy(pressed.at[pl.ds(0, ready)], out_p.at[pl.ds(0, ready)], sem.at[3])]
    for copy in early:
        copy.start()

    def w(c, x):
        return nW[c, x - a] if a <= x < b else W[c, x + 1]

    def change(x):
        return n1[x - a] if a <= x < nx - 1 else c1[x + 1, 0:ny]

    def second(x):
        return n2[x - (a - 1)] if a - 1 <= x < nx else c2[x]

    for x in range(a, b):
        for c in range(3):
            nW[c, x - a, 0:2] = W[c, x + 1, 0:2]
            nW[c, x - a, ny - 2 : ny] = W[c, x + 1, ny - 2 : ny]
            for p in range(parts):
                t = 2 + 4 * p
                nW[c, x - a, t : t + 4] = W[c, x + 1, t : t + 4] + C[c, x + 1, t : t + 4] * rL[x - a, p, c]
    for x in range(a, nx - 1):
        n1[x - a] = first_change(SC[x], S[x], w(0, x), w(0, x - 1), w(1, x), up_r[0, x], w(2, x))
    for x in range(a - 1, nx):
        e = x + 1
        n2[x - (a - 1)] = second_change(
            SC[x], change(x), change(x + 1), change(x - 1), c1[e, ny : ny + 1], up_r[1, x],
            C[0, e], C[0, x], C[1, e], Ch[x], C[2, e],
        )
    for x in range(ready, nx):
        e = x + 1
        here = second(x)
        nP[x - ready] = Pr[x] + here
        fresh = final_velocity(
            [w(c, x) for c in range(3)], [C[c, e] for c in range(3)], here, second(x + 1), c2e[x]
        )
        for c in range(3):
            nV[c, x - ready] = fresh[c]
    late = [
        pltpu.make_async_copy(nV.at[c], out_v.at[c, pl.ds(ready, nx - ready)], sem.at[4 + c]) for c in range(3)
    ] + [pltpu.make_async_copy(nP, out_p.at[pl.ds(ready, nx - ready)], sem.at[7])]
    for copy in late:
        copy.start()
    for copy in early + late:
        copy.wait()


def body(counts, velocity, pressure, forcing, source, viscosity):
    _, steps, nx, ny, nz = velocity.shape
    assert steps == 1 and nx >= 8 and ny >= 8 and ny % 4 == 0
    groups = [(0, 2), (nx - 2, nx), (2, 4)] + groups_of(4, nx - 4, 4) + [(nx - 4, nx - 2)]
    detour = (1, 3, 2, 2) if counts[0] == 4 else None
    last = groups[-1]
    parts = (ny - 4) // 4
    vmem = lambda *shape: pltpu.VMEM(shape, jnp.float32)
    rows = lambda *lead: vmem(*lead, nx, 1, nz)
    any_space = pl.BlockSpec(memory_space=pl.ANY)
    on_chip = pl.BlockSpec(memory_space=pltpu.VMEM)
    kept = (
        vmem(3, nx, ny, nz), vmem(nx, ny, nz), vmem(last[1] - last[0], parts, 3, 4, nz),
        vmem(3, nx + 1, ny, nz), vmem(3, nx + 1, ny, nz), vmem(nx + 2, ny + 8, nz), vmem(nx + 1, ny, nz), rows(),
        vmem(nx, ny, nz), vmem(nx, ny, nz), vmem(nx + 1, ny, nz), rows(2), rows(),
    )
    inputs = (velocity[:, 0], pressure[0], forcing[:, 0], source[0], viscosity)
    held = pl.pallas_call(
        functools.partial(kernel, *counts, groups, detour),
        out_shape=kept,
        in_specs=[any_space] * 5,
        out_specs=(on_chip,) * len(kept),
        scratch_shapes=[
            vmem(3, nx + 2, ny, nz), vmem(3, nx, ny, nz), vmem(3, nx + 1, ny, nz),
            vmem(3, nx, 4, nz), vmem(3, nx, 4, nz),
            vmem(nx, parts, 3, 4, nz), vmem(nx, parts, 3, 4, nz), vmem(2, parts, 3, 4, nz),
            rows(4), rows(4), rows(4), rows(4), vmem(4, nx + 1, 1, nz), rows(4),
            vmem(ny, nz), vmem(ny, nz), rows(2), rows(2), rows(2),
            pltpu.SemaphoreType.DMA((5,)),
            pltpu.SemaphoreType.DMA((17 + len(groups),)),
            pltpu.SemaphoreType.DMA((17 + len(groups),)),
        ],
        compiler_params=pltpu.CompilerParams(
            collective_id=0, has_side_effects=True, vmem_limit_bytes=40 << 20
        ),
        name="smoother",
    )(*(pltpu.with_memory_space_constraint(a, pltpu.HBM) for a in inputs))
    out_v, out_p = pl.pallas_call(
        functools.partial(settle, last),
        out_shape=(
            jax.ShapeDtypeStruct((3, nx, ny, nz), jnp.float32),
            jax.ShapeDtypeStruct((nx, ny, nz), jnp.float32),
        ),
        in_specs=[on_chip] * len(kept),
        out_specs=(any_space, any_space),
        scratch_shapes=[
            vmem(3, 6, ny, nz), vmem(6, ny, nz), vmem(3, 2, ny, nz), vmem(3, ny, nz), vmem(5, ny, nz),
            pltpu.SemaphoreType.DMA((8,)),
        ],
        compiler_params=pltpu.CompilerParams(vmem_limit_bytes=2 << 20),
        name="settle",
    )(*held)
    return out_v[:, None], out_p[None]


def solution(mesh):
    placed = (
        P(None, "ta", "gx", "gy", None),
        P("ta", "gx", "gy", None),
        P(None, "ta", "gx", "gy", None),
        P("ta", "gx", "gy", None),
        P(None, "gx", "gy", None),
    )
    counts = tuple(mesh.shape[axis] for axis in ("ta", "gx", "gy"))
    return jax.shard_map(
        functools.partial(body, counts),
        mesh=mesh,
        in_specs=placed,
        out_specs=(P(None, "ta", "gx", "gy", None), P("ta", "gx", "gy", None)),
        check_vma=False,
    )
```

time: 25.6 us -> 22.3 us (0.87)
  Pallas kernels: 24.8 us -> 21.6 us
    pallas_call x2, Pallas kernels: 24.8 us -> 21.6 us  [the longest x1 20.3 us: body(): pl.pallas_call(functools.partial(kernel, *counts, groups, detour), out_sh...]
where the time goes in v2:
time: 22.3 us; the launch traced here: 22.2 us
  Pallas kernels  21.6 us (97%)
  between operations  0.64 us (3%)
    pallas_call x1, Pallas kernels, body(): pl.pallas_call(functools.partial(kernel, *counts, groups, detour), out_sh...  20.3 us
    pallas_call x1, Pallas kernels, body(): pl.pallas_call(functools.partial(settle, last), out_shape=(jax.ShapeDtype...  1.23 us

profile of v2, /device:TPU:0, one launch (start us, length us, event | category | flops | bytes accessed | tf_op | source)
XLA Modules:
  0.0 22.2 jit_solution(15466427255609213098)
XLA Ops:
  0.6 20.3 %smoother.1 = (f32[3,16,16,256]{3,2,1,0:T(8,128)S(1)}, f32[16,16,256]{2,1,0:T(8,128)S(1)}, f32[2,3,3,4,256]{4,3,2,1,0:T(4,128)S(1)}, f32[3,17,16,256]{3,2,1,0:T(...) custom-call(f32[3,16,16,256]{3,2,1,0:T(8,128)} %bitcast.8, ...), custom_call_target="tpu_custom_call" | custom-call | tf_op jit(solution)/shard_map/smoother/pallas_call | solution.py:481
  21.0 1.2 %settle.1 = (f32[3,16,16,256]{3,2,1,0:T(8,128)}, f32[16,16,256]{2,1,0:T(8,128)}) custom-call(f32[3,16,16,256]{3,2,1,0:T(8,128)S(1)} %get-tuple-element.17.moved, f32[16,16,256]{2,1,0:T(8,128)S(1)} %get-tuple-element.18.pressed, f32[2,3,3,4,256]{4,3,2,1,0:T(4,128)S(1)} %get-tuple-element.19.rL, f32[3,17,16,256]{3,2,1,0:T(8,128)S(1)} %get-tuple-element.20.W, ...), custom_call_target="tpu_custom_call" | custom-call | tf_op jit(solution)/shard_map/settle/pallas_call | solution.py:501

commit v3 on v2

--- a/solution.py
+++ b/solution.py
@@ -75,7 +75,7 @@
     slabs, nx_parts, ny_parts, groups, detour,
     vel, prs, frc, src, vis,
     OV, OP, rL, W, C, c1, c2, c2e, SC, S, Pr, up_r, Ch,
-    V, F, Nu, sE, rE, sI, rI, rR, yu_s, yd_s, yu_r, yd_r, Ce, m_s, fe_s, fe_r, up_s, dn_s, dn_r,
+    V, F, Nu, sE, rE, sI, rI, rR, yu_s, yd_s, yu_r, yd_r, Ce, m_s, fe_s, fe_r, up_s, dn_s, dn_r, tally,
     load_sem, send_sem, recv_sem,
 ):
     _, nx, ny, nz = vel.shape
@@ -88,16 +88,6 @@
     yu, yd = lax.rem(gy + 1, ny_parts), lax.rem(gy + ny_parts - 1, ny_parts)
     first_row = gy == 0
 
-    loads = [
-        pltpu.make_async_copy(vel, V.at[:, pl.ds(1, nx)], load_sem.at[0]),
-        pltpu.make_async_copy(vis, Nu.at[:, pl.ds(1, nx)], load_sem.at[1]),
-        pltpu.make_async_copy(prs, Pr.at[pl.ds(0, nx)], load_sem.at[2]),
-        pltpu.make_async_copy(frc, F, load_sem.at[3]),
-        pltpu.make_async_copy(src, S, load_sem.at[4]),
-    ]
-    for copy in loads:
-        copy.start()
-
     barrier = pltpu.get_barrier_semaphore()
 
     def greet(axis, index):
@@ -130,34 +120,50 @@
         def _():
             greet("gy", beside)
 
-    def remote(k, source, target, axis, index):
+    def fetch(source, target, k):
+        pltpu.make_async_copy(source, target, load_sem.at[k]).start()
+
+    def wait_rows(sem, count):
+        size = pl.ds(0, count)
+        pltpu.make_async_copy(tally.at[size], tally.at[size], sem).wait()
+
+    half = nx // 2
+    for a, n in ((0, half), (half, nx - half)):
+        for c in range(3):
+            fetch(vel.at[c, pl.ds(a, n)], V.at[c, pl.ds(1 + a, n)], 0)
+    fetch(vis, Nu.at[:, pl.ds(1, nx)], 1)
+    fetch(prs, Pr.at[pl.ds(0, nx)], 1)
+    fetch(frc, F, 2)
+    fetch(src, S, 2)
+
+    def remote(send, recv, source, target, axis, index):
         return pltpu.make_async_remote_copy(
-            src_ref=source, dst_ref=target, send_sem=send_sem.at[k], recv_sem=recv_sem.at[k],
+            src_ref=source, dst_ref=target, send_sem=send_sem.at[send], recv_sem=recv_sem.at[recv],
             device_id={axis: index}, device_id_type=MESH,
         )
 
-    vx_up = remote(0, V.at[:, nx], V.at[:, 0], "gx", xu)
-    vx_dn = remote(1, V.at[:, 1], V.at[:, nx + 1], "gx", xd)
-    px_dn = remote(2, Pr.at[0], Pr.at[nx], "gx", xd)
-    nx_up = remote(3, Nu.at[0, nx], Nu.at[0, 0], "gx", xu)
-    ry_up = remote(4, yu_s, yu_r, "gy", yu)
-    ry_dn = remote(5, yd_s, yd_r, "gy", yd)
-    fe_up = remote(6, fe_s, fe_r, "gx", xu)
-    fx_up = remote(7, W.at[0, nx], W.at[0, 0], "gx", xu)
-    cx_dn = remote(8, c1.at[1], c1.at[nx + 1], "gx", xd)
-    cx_up = remote(9, c1.at[nx], c1.at[0], "gx", xu)
-    m_dn = remote(10, m_s, Ce.at[:, pl.ds(1, nx)], "gy", yd)
-    ce_up = remote(11, Ce.at[0, nx], Ce.at[0, 0], "gx", xu)
-    y_up = remote(12, up_s, up_r, "gy", yu)
-    y_dn = remote(13, dn_s, dn_r, "gy", yd)
-    ex_dn = remote(14, c2.at[0], c2.at[nx], "gx", xd)
-    edge = remote(15, sE, rE, "ta", t_next)
+    vx_up = remote(0, 0, V.at[:, nx], V.at[:, 0], "gx", xu)
+    vx_dn = remote(0, 0, V.at[:, 1], V.at[:, nx + 1], "gx", xd)
+    px_dn = remote(0, 0, Pr.at[0], Pr.at[nx], "gx", xd)
+    nx_up = remote(0, 0, Nu.at[0, nx], Nu.at[0, 0], "gx", xu)
+    ry_up = remote(0, 0, yu_s, yu_r, "gy", yu)
+    ry_dn = remote(0, 0, yd_s, yd_r, "gy", yd)
+    fe_up = remote(0, 1, fe_s, fe_r, "gx", xu)
+    fx_up = remote(0, 3, W.at[0, nx], W.at[0, 0], "gx", xu)
+    cx_dn = remote(0, 4, c1.at[1], c1.at[nx + 1], "gx", xd)
+    cx_up = remote(0, 4, c1.at[nx], c1.at[0], "gx", xu)
+    m_dn = remote(0, 2, m_s, Ce.at[:, pl.ds(1, nx)], "gy", yd)
+    ce_up = remote(3, 5, Ce.at[0, nx], Ce.at[0, 0], "gx", xu)
+    y_up = remote(0, 3, up_s, up_r, "gy", yu)
+    y_dn = remote(0, 3, dn_s, dn_r, "gy", yd)
+    ex_dn = remote(0, 6, c2.at[0], c2.at[nx], "gx", xd)
+    edge = remote(1, 7, sE, rE, "ta", t_next)
     landing = [rI.at[pl.ds(a, b - a)] for a, b in groups[:final]] + [rL]
     leaving = [sI.at[pl.ds(a, b - a)] for a, b in groups]
-    pieces = [remote(16 + k, leaving[k], landing[k], "ta", t_next) for k in range(final + 1)]
+    pieces = [remote(1, 8 + k, leaving[k], landing[k], "ta", t_next) for k in range(final + 1)]
     if detour:
-        to_via = remote(17 + final, leaving[lane], rR, "ta", via)
-        from_via = remote(16 + lane, rR, landing[lane], "ta", taker)
+        to_via = remote(1, 9 + final, leaving[lane], rR, "ta", via)
+        from_via = remote(2, 8 + lane, rR, landing[lane], "ta", taker)
 
     def pack_edges(x):
         for c in range(3):
@@ -176,7 +182,7 @@
             for p in range(parts):
                 sI[x, p, c] = V[c, x + 1, 2 + 4 * p : 6 + 4 * p]
 
-    loads[0].wait()
+    wait_rows(load_sem.at[0], 3 * nx * ny)
     loop(0, nx, pack_edges)
     pl.semaphore_wait(barrier, expected)
     for beside in (yu, yd):
@@ -189,8 +195,7 @@
     def _():
         edge.start()
 
-    loads[1].wait()
-    loads[2].wait()
+    wait_rows(load_sem.at[1], 4 * nx * ny)
     loop(0, nx, pack_rows)
     for copy in (vx_up, vx_dn, px_dn, nx_up):
         copy.start()
@@ -224,10 +229,8 @@
         ry_up.start()
         ry_dn.start()
 
-    loads[3].wait()
-    loads[4].wait()
-    for copy in (vx_up, vx_dn, px_dn, nx_up, ry_up, ry_dn):
-        copy.wait_recv()
+    wait_rows(load_sem.at[2], 4 * nx * ny)
+    wait_rows(recv_sem.at[0], 8 * (ny + nx))
     C[0, 0] = coeff_of(Nu[0, 0])
 
     def prepare(x):
@@ -307,8 +310,7 @@
     fx_up.start()
     m_dn.wait_recv()
     ce_up.start()
-    for copy in (fx_up, y_up, y_dn):
-        copy.wait_recv()
+    wait_rows(recv_sem.at[3], ny + 4 * nx)
 
     def first(x):
         e = x + 1
@@ -322,8 +324,8 @@
     loop(0, nx, first_above)
     for copy in (cx_dn, cx_up):
         copy.start()
-    for copy in (cx_dn, cx_up, ce_up):
-        copy.wait_recv()
+    wait_rows(recv_sem.at[4], 2 * (ny + 8))
+    ce_up.wait_recv()
 
     def second(x):
         e = x + 1
@@ -377,20 +379,7 @@
 
     @pl.when(has_next)
     def _():
-        edge.wait_send()
-        for k, copy in enumerate(pieces):
-            if detour and k == lane:
-
-                @pl.when(ta == giver)
-                def _():
-                    to_via.wait_send()
-
-                @pl.when(ta != giver)
-                def _():
-                    copy.wait_send()
-
-            else:
-                copy.wait_send()
+        wait_rows(send_sem.at[1], 3 * nx * ny)
 
     if detour:
 
@@ -398,10 +387,8 @@
         def _():
             from_via.wait_send()
 
-    for copy in (
-        vx_up, vx_dn, px_dn, nx_up, ry_up, ry_dn, fe_up, fx_up, cx_dn, cx_up, m_dn, ce_up, y_up, y_dn, ex_dn
-    ):
-        copy.wait_send()
+    ce_up.wait_send()
+    wait_rows(send_sem.at[0], 13 * ny + 16 + 16 * nx)
 
 
 def settle(
@@ -428,35 +415,39 @@
     def second(x):
         return n2[x - (a - 1)] if a - 1 <= x < nx else c2[x]
 
-    for x in range(a, b):
-        for c in range(3):
-            nW[c, x - a, 0:2] = W[c, x + 1, 0:2]
-            nW[c, x - a, ny - 2 : ny] = W[c, x + 1, ny - 2 : ny]
-            for p in range(parts):
-                t = 2 + 4 * p
-                nW[c, x - a, t : t + 4] = W[c, x + 1, t : t + 4] + C[c, x + 1, t : t + 4] * rL[x - a, p, c]
-    for x in range(a, nx - 1):
-        n1[x - a] = first_change(SC[x], S[x], w(0, x), w(0, x - 1), w(1, x), up_r[0, x], w(2, x))
-    for x in range(a - 1, nx):
-        e = x + 1
-        n2[x - (a - 1)] = second_change(
-            SC[x], change(x), change(x + 1), change(x - 1), c1[e, ny : ny + 1], up_r[1, x],
-            C[0, e], C[0, x], C[1, e], Ch[x], C[2, e],
-        )
-    for x in range(ready, nx):
-        e = x + 1
-        here = second(x)
-        nP[x - ready] = Pr[x] + here
-        fresh = final_velocity(
-            [w(c, x) for c in range(3)], [C[c, e] for c in range(3)], here, second(x + 1), c2e[x]
-        )
-        for c in range(3):
-            nV[c, x - ready] = fresh[c]
     late = [
         pltpu.make_async_copy(nV.at[c], out_v.at[c, pl.ds(ready, nx - ready)], sem.at[4 + c]) for c in range(3)
     ] + [pltpu.make_async_copy(nP, out_p.at[pl.ds(ready, nx - ready)], sem.at[7])]
-    for copy in late:
-        copy.start()
+
+    @pl.when(lax.axis_index("ta") >= 0)
+    def _():
+        for x in range(a, b):
+            for c in range(3):
+                nW[c, x - a, 0:2] = W[c, x + 1, 0:2]
+                nW[c, x - a, ny - 2 : ny] = W[c, x + 1, ny - 2 : ny]
+                for p in range(parts):
+                    t = 2 + 4 * p
+                    nW[c, x - a, t : t + 4] = W[c, x + 1, t : t + 4] + C[c, x + 1, t : t + 4] * rL[x - a, p, c]
+        for x in range(a, nx - 1):
+            n1[x - a] = first_change(SC[x], S[x], w(0, x), w(0, x - 1), w(1, x), up_r[0, x], w(2, x))
+        for x in range(a - 1, nx):
+            e = x + 1
+            n2[x - (a - 1)] = second_change(
+                SC[x], change(x), change(x + 1), change(x - 1), c1[e, ny : ny + 1], up_r[1, x],
+                C[0, e], C[0, x], C[1, e], Ch[x], C[2, e],
+            )
+        for x in range(ready, nx):
+            e = x + 1
+            here = second(x)
+            nP[x - ready] = Pr[x] + here
+            fresh = final_velocity(
+                [w(c, x) for c in range(3)], [C[c, e] for c in range(3)], here, second(x + 1), c2e[x]
+            )
+            for c in range(3):
+                nV[c, x - ready] = fresh[c]
+        for copy in late:
+            copy.start()
+
     for copy in early + late:
         copy.wait()
 
@@ -488,10 +479,10 @@
             vmem(3, nx, 4, nz), vmem(3, nx, 4, nz),
             vmem(nx, parts, 3, 4, nz), vmem(nx, parts, 3, 4, nz), vmem(2, parts, 3, 4, nz),
             rows(4), rows(4), rows(4), rows(4), vmem(4, nx + 1, 1, nz), rows(4),
-            vmem(ny, nz), vmem(ny, nz), rows(2), rows(2), rows(2),
-            pltpu.SemaphoreType.DMA((5,)),
-            pltpu.SemaphoreType.DMA((17 + len(groups),)),
-            pltpu.SemaphoreType.DMA((17 + len(groups),)),
+            vmem(ny, nz), vmem(ny, nz), rows(2), rows(2), rows(2), vmem(4 * nx * ny, nz),
+            pltpu.SemaphoreType.DMA((3,)),
+            pltpu.SemaphoreType.DMA((4,)),
+            pltpu.SemaphoreType.DMA((9 + len(groups),)),
         ],
         compiler_params=pltpu.CompilerParams(
             collective_id=0, has_side_effects=True, vmem_limit_bytes=40 << 20

time: 22.3 us -> 22 us (0.987)
  the two profiles are of different devices: /device:TPU:0 before, /device:TPU:14 now
where the time goes in v3:
time: 22 us; the launch traced here: 21.6 us
  Pallas kernels  21 us (95%)
  between operations  0.64 us (3%)
    pallas_call x1, Pallas kernels, body(): pl.pallas_call(functools.partial(kernel, *counts, groups, detour), out_sh...  19.8 us
    pallas_call x1, Pallas kernels, body(): pl.pallas_call(functools.partial(settle, last), out_shape=(jax.ShapeDtype...  1.21 us

profile of v3, /device:TPU:14, one launch (start us, length us, event | category | flops | bytes accessed | tf_op | source)
XLA Modules:
  0.0 21.6 jit_solution(716207740965395409)
XLA Ops:
  0.6 19.8 %smoother.1 = (f32[3,16,16,256]{3,2,1,0:T(8,128)S(1)}, f32[16,16,256]{2,1,0:T(8,128)S(1)}, f32[2,3,3,4,256]{4,3,2,1,0:T(4,128)S(1)}, f32[3,17,16,256]{3,2,1,0:T(...) custom-call(f32[3,16,16,256]{3,2,1,0:T(8,128)} %bitcast.8, ...), custom_call_target="tpu_custom_call" | custom-call | tf_op jit(solution)/shard_map/smoother/pallas_call | solution.py:472
  20.4 1.2 %settle.1 = (f32[3,16,16,256]{3,2,1,0:T(8,128)}, f32[16,16,256]{2,1,0:T(8,128)}) custom-call(f32[3,16,16,256]{3,2,1,0:T(8,128)S(1)} %get-tuple-element.17.moved, f32[16,16,256]{2,1,0:T(8,128)S(1)} %get-tuple-element.18.pressed, f32[2,3,3,4,256]{4,3,2,1,0:T(4,128)S(1)} %get-tuple-element.19.rL, f32[3,17,16,256]{3,2,1,0:T(8,128)S(1)} %get-tuple-element.20.W, ...), custom_call_target="tpu_custom_call" | custom-call | tf_op jit(solution)/shard_map/settle/pallas_call | solution.py:492

commit v4 on v3

--- a/solution.py
+++ b/solution.py
@@ -75,7 +75,7 @@
     slabs, nx_parts, ny_parts, groups, detour,
     vel, prs, frc, src, vis,
     OV, OP, rL, W, C, c1, c2, c2e, SC, S, Pr, up_r, Ch,
-    V, F, Nu, sE, rE, sI, rI, rR, yu_s, yd_s, yu_r, yd_r, Ce, m_s, fe_s, fe_r, up_s, dn_s, dn_r, tally,
+    V, F, Nu, sE, rE, sI, rI, rR, yu_s, yd_s, yu_r, yd_r, Ce, m_s, fe_s, fe_r, up_s, dn_s, dn_r, Se, tally,
     load_sem, send_sem, recv_sem,
 ):
     _, nx, ny, nz = vel.shape
@@ -93,9 +93,6 @@
     def greet(axis, index):
         pl.semaphore_signal(barrier, inc=1, device_id={axis: index}, device_id_type=MESH)
 
-    greet("gx", xu)
-    greet("gx", xd)
-
     @pl.when(has_prev)
     def _():
         greet("ta", t_prev)
@@ -114,12 +111,6 @@
 
         expected = expected + ((ta == giver) | (ta == via)).astype(jnp.int32)
 
-    for beside in (yu, yd):
-
-        @pl.when(jnp.logical_not(first_row) & (beside != 0))
-        def _():
-            greet("gy", beside)
-
     def fetch(source, target, k):
         pltpu.make_async_copy(source, target, load_sem.at[k]).start()
 
@@ -131,10 +122,20 @@
     for a, n in ((0, half), (half, nx - half)):
         for c in range(3):
             fetch(vel.at[c, pl.ds(a, n)], V.at[c, pl.ds(1 + a, n)], 0)
-    fetch(vis, Nu.at[:, pl.ds(1, nx)], 1)
+    for c in range(3):
+        fetch(vis.at[c], Nu.at[c, pl.ds(1, nx)], 1)
     fetch(prs, Pr.at[pl.ds(0, nx)], 1)
-    fetch(frc, F, 2)
+    for c in range(3):
+        fetch(frc.at[c], F.at[c], 2)
     fetch(src, S, 2)
+
+    greet("gx", xu)
+    greet("gx", xd)
+    for beside in (yu, yd):
+
+        @pl.when(jnp.logical_not(first_row) & (beside != 0))
+        def _():
+            greet("gy", beside)
 
     def remote(send, recv, source, target, axis, index):
         return pltpu.make_async_remote_copy(
@@ -146,8 +147,11 @@
     vx_dn = remote(0, 0, V.at[:, 1], V.at[:, nx + 1], "gx", xd)
     px_dn = remote(0, 0, Pr.at[0], Pr.at[nx], "gx", xd)
     nx_up = remote(0, 0, Nu.at[0, nx], Nu.at[0, 0], "gx", xu)
-    ry_up = remote(0, 0, yu_s, yu_r, "gy", yu)
-    ry_dn = remote(0, 0, yd_s, yd_r, "gy", yd)
+    three, fourth = pl.ds(0, 3), pl.ds(3, 1)
+    ry_up = remote(0, final + 9, yu_s.at[three], yu_r.at[three], "gy", yu)
+    ry_dn = remote(0, final + 9, yd_s.at[three], yd_r.at[three], "gy", yd)
+    rz_up = remote(0, final + 9, yu_s.at[fourth], yu_r.at[fourth], "gy", yu)
+    rz_dn = remote(0, final + 9, yd_s.at[fourth], yd_r.at[fourth], "gy", yd)
     fe_up = remote(0, 1, fe_s, fe_r, "gx", xu)
     fx_up = remote(0, 3, W.at[0, nx], W.at[0, 0], "gx", xu)
     cx_dn = remote(0, 4, c1.at[1], c1.at[nx + 1], "gx", xd)
@@ -158,11 +162,11 @@
     y_dn = remote(0, 3, dn_s, dn_r, "gy", yd)
     ex_dn = remote(0, 6, c2.at[0], c2.at[nx], "gx", xd)
     edge = remote(1, 7, sE, rE, "ta", t_next)
-    landing = [rI.at[pl.ds(a, b - a)] for a, b in groups[:final]] + [rL]
-    leaving = [sI.at[pl.ds(a, b - a)] for a, b in groups]
+    landing = [rI.at[pl.ds(a, b - a), pl.ds(p, q - p)] for a, b, p, q in groups[:final]] + [rL]
+    leaving = [sI.at[pl.ds(a, b - a), pl.ds(p, q - p)] for a, b, p, q in groups]
     pieces = [remote(1, 8 + k, leaving[k], landing[k], "ta", t_next) for k in range(final + 1)]
     if detour:
-        to_via = remote(1, 9 + final, leaving[lane], rR, "ta", via)
+        to_via = remote(1, 10 + final, leaving[lane], rR, "ta", via)
         from_via = remote(2, 8 + lane, rR, landing[lane], "ta", taker)
 
     def pack_edges(x):
@@ -174,6 +178,8 @@
         for c in range(3):
             yu_s[c, x] = V[c, x + 1, ny - 1 : ny]
             yd_s[c, x] = V[c, x + 1, 0:1]
+
+    def pack_more(x):
         yu_s[3, x] = Nu[1, x + 1, ny - 1 : ny]
         yd_s[3, x] = Pr[x, 0:1]
 
@@ -185,25 +191,35 @@
     wait_rows(load_sem.at[0], 3 * nx * ny)
     loop(0, nx, pack_edges)
     pl.semaphore_wait(barrier, expected)
+
+    @pl.when(has_next)
+    def _():
+        edge.start()
+
     for beside in (yu, yd):
 
         @pl.when(first_row | (beside == 0))
         def _():
             greet("gy", beside)
 
-    @pl.when(has_next)
-    def _():
-        edge.start()
-
-    wait_rows(load_sem.at[1], 4 * nx * ny)
     loop(0, nx, pack_rows)
-    for copy in (vx_up, vx_dn, px_dn, nx_up):
+    for copy in (vx_up, vx_dn):
         copy.start()
 
     @pl.when(jnp.logical_not(first_row))
     def _():
         ry_up.start()
         ry_dn.start()
+
+    wait_rows(load_sem.at[1], 4 * nx * ny)
+    loop(0, nx, pack_more)
+    for copy in (px_dn, nx_up):
+        copy.start()
+
+    @pl.when(jnp.logical_not(first_row))
+    def _():
+        rz_up.start()
+        rz_dn.start()
 
     loop(0, nx, pack_inner)
 
@@ -226,36 +242,48 @@
     @pl.when(first_row)
     def _():
         pl.semaphore_wait(barrier, 2)
-        ry_up.start()
-        ry_dn.start()
+        for copy in (ry_up, ry_dn, rz_up, rz_dn):
+            copy.start()
 
     wait_rows(load_sem.at[2], 4 * nx * ny)
-    wait_rows(recv_sem.at[0], 8 * (ny + nx))
+    wait_rows(recv_sem.at[0], 8 * ny)
     C[0, 0] = coeff_of(Nu[0, 0])
 
     def prepare(x):
         e = x + 1
-        below = coeff_of(yu_r[3, x])
-        Ch[x] = below
+        none = jnp.zeros((1, nz), jnp.float32)
         coeff = [coeff_of(Nu[c, e]) for c in range(3)]
         for c in range(3):
             C[c, e] = coeff[c]
             m_s[c, x] = coeff[c][0:1]
-        total = coeff[0] + C[0, x] + coeff[1] + y_last(coeff[1], below) + coeff[2] + z_last(coeff[2])
-        scale = damping / total
-        SC[x] = scale
-        m_s[3, x] = scale[0:1]
+        total = coeff[0] + C[0, x] + coeff[1] + y_last(coeff[1], none) + coeff[2] + z_last(coeff[2])
+        SC[x] = damping / total
+        m_s[3, x] = total[0:1]
         press = Pr[x]
-        grads = (Pr[x + 1] - press, y_next(press, yd_r[3, x]) - press, z_next(press) - press)
+        grads = (Pr[x + 1] - press, y_next(press, none) - press, z_next(press) - press)
         for c in range(3):
             v = V[c, e]
-            near = V[c, e - 1] + V[c, e + 1] + y_last(v, yu_r[c, x]) + y_next(v, yd_r[c, x])
+            near = V[c, e - 1] + V[c, e + 1] + y_last(v, none) + y_next(v, none)
             near = near + z_last(v) + z_next(v)
             momentum = F[c, x] - (v + Nu[c, e] * (6.0 * v - near)) - grads[c]
             W[c, e] = v + coeff[c] * momentum
 
+    def complete(x):
+        e, t = x + 1, ny - 1
+        below = coeff_of(yu_r[3, x])
+        Ch[x] = below
+        SC[x, 0:1] = damping / (m_s[3, x] + below)
+        for c in range(3):
+            W[c, e, 0:1] = W[c, e, 0:1] + C[c, e, 0:1] * (Nu[c, e, 0:1] * yu_r[c, x])
+            more = Nu[c, e, t:ny] * yd_r[c, x]
+            if c == 1:
+                more = more - yd_r[3, x]
+            W[c, e, t:ny] = W[c, e, t:ny] + C[c, e, t:ny] * more
+
     loop(0, nx, prepare)
     m_dn.start()
+    wait_rows(recv_sem.at[final + 9], 8 * nx)
+    loop(0, nx, complete)
     if detour:
 
         @pl.when(ta == via)
@@ -270,9 +298,9 @@
                     W[c, x + 1, t : t + 2] + C[c, x + 1, t : t + 2] * rE[c, x, s : s + 2]
                 )
 
-    def add_inner(x):
-        for c in range(3):
-            for p in range(parts):
+    def add_inner(x, first_part, parts_end):
+        for c in range(3):
+            for p in range(first_part, parts_end):
                 t = 2 + 4 * p
                 W[c, x + 1, t : t + 4] = W[c, x + 1, t : t + 4] + C[c, x + 1, t : t + 4] * rI[x, p, c]
 
@@ -280,7 +308,8 @@
         @pl.when(has_prev)
         def _():
             pieces[k].wait_recv()
-            loop(*groups[k], add_inner)
+            a, b, p, q = groups[k]
+            loop(a, b, lambda x: add_inner(x, p, q))
 
     @pl.when(has_prev)
     def _():
@@ -318,12 +347,17 @@
 
     def first_above(x):
         e = x + 1
-        c1[e, ny : ny + 1] = dn_r[0, x] + Ce[3, e] * W[1, e, ny - 1 : ny]
-
-    loop(0, nx, first)
-    loop(0, nx, first_above)
+        scale = damping / (Ce[3, e] + C[1, e, ny - 1 : ny])
+        Se[x] = scale
+        c1[e, ny : ny + 1] = dn_r[0, x] + scale * W[1, e, ny - 1 : ny]
+
+    for x in (0, nx - 1):
+        first(x)
+        first_above(x)
     for copy in (cx_dn, cx_up):
         copy.start()
+    loop(1, nx - 1, first)
+    loop(1, nx - 1, first_above)
     wait_rows(recv_sem.at[4], 2 * (ny + 8))
     ce_up.wait_recv()
 
@@ -344,7 +378,7 @@
         g1_last = wide(C[1, e, ny - 1 : ny]) * (here - wide(c1[e, ny - 1 : ny]))
         g2 = wide(Ce[2, e]) * (z_next(here) - here)
         div = (g0 - g0_last) + (g1 - g1_last) + (g2 - z_last(g2))
-        c2e[x] = (2.0 * here + wide(Ce[3, e]) * div)[0:1]
+        c2e[x] = (2.0 * here + wide(Se[x]) * div)[0:1]
 
     second(0)
     ex_dn.start()
@@ -360,22 +394,38 @@
         for c in range(3):
             OV[c, x] = moved[c]
 
-    for k in range(2, final):
-        a, b = groups[k]
+    def finish_low(x):
+        e, low = x + 1, slice(0, ny - 8)
+        here = c2[x, low]
+        OP[x, low] = Pr[x, low] + here
+        moved = final_velocity(
+            [W[c, e, low] for c in range(3)], [C[c, e, low] for c in range(3)], here, c2[x + 1, low],
+            c2[x, ny - 8 : ny - 7],
+        )
+        for c in range(3):
+            OV[c, x, low] = moved[c]
+
+    for k in range(2, final - 1):
+        a, b, _, _ = groups[k]
         arrive(k)
         loop(a, b, first)
         loop(a - 1, b - 1, second)
         loop(a - 2, b - 2, finish)
 
+    @pl.when(jnp.logical_not(has_prev))
+    def _():
+        rL[...] = jnp.zeros_like(rL)
+
     ex_dn.wait_recv()
+    a = groups[final][0]
+    arrive(final - 1)
+    loop(a, nx - 1, first)
+    loop(a - 1, nx, second)
+    loop(a - 2, nx, finish_low)
 
     @pl.when(has_prev)
     def _():
         pieces[final].wait_recv()
-
-    @pl.when(jnp.logical_not(has_prev))
-    def _():
-        rL[...] = jnp.zeros_like(rL)
 
     @pl.when(has_next)
     def _():
@@ -395,76 +445,72 @@
     last, moved, pressed, rL, W, C, c1, c2, c2e, SC, S, Pr, up_r, Ch, out_v, out_p, nV, nP, nW, n1, n2, sem
 ):
     _, nx, ny, nz = out_v.shape
-    parts = (ny - 4) // 4
     a, b = last
-    ready = a - 2
-
-    early = [
-        pltpu.make_async_copy(moved.at[c, pl.ds(0, ready)], out_v.at[c, pl.ds(0, ready)], sem.at[c])
-        for c in range(3)
-    ] + [pltpu.make_async_copy(pressed.at[pl.ds(0, ready)], out_p.at[pl.ds(0, ready)], sem.at[3])]
-    for copy in early:
-        copy.start()
+    ready, u = a - 2, ny - 8
+    done, rest = pl.ds(0, ready), pl.ds(ready, nx - ready)
+    low, top = pl.ds(0, u), pl.ds(u, 8)
+
+    for c in range(3):
+        pltpu.make_async_copy(moved.at[c, done], out_v.at[c, done], sem.at[0]).start()
+        pltpu.make_async_copy(moved.at[c, rest, low], out_v.at[c, rest, low], sem.at[0]).start()
+    pltpu.make_async_copy(pressed.at[done], out_p.at[done], sem.at[1]).start()
+    pltpu.make_async_copy(pressed.at[rest, low], out_p.at[rest, low], sem.at[1]).start()
 
     def w(c, x):
-        return nW[c, x - a] if a <= x < b else W[c, x + 1]
+        return nW[c, x - a] if a <= x < b else W[c, x + 1, u:ny]
 
     def change(x):
-        return n1[x - a] if a <= x < nx - 1 else c1[x + 1, 0:ny]
+        return n1[x - a] if a <= x < nx - 1 else c1[x + 1, u:ny]
 
     def second(x):
-        return n2[x - (a - 1)] if a - 1 <= x < nx else c2[x]
-
-    late = [
-        pltpu.make_async_copy(nV.at[c], out_v.at[c, pl.ds(ready, nx - ready)], sem.at[4 + c]) for c in range(3)
-    ] + [pltpu.make_async_copy(nP, out_p.at[pl.ds(ready, nx - ready)], sem.at[7])]
+        return n2[x - (a - 1)] if a - 1 <= x < nx else c2[x, u:ny]
 
     @pl.when(lax.axis_index("ta") >= 0)
     def _():
         for x in range(a, b):
             for c in range(3):
-                nW[c, x - a, 0:2] = W[c, x + 1, 0:2]
-                nW[c, x - a, ny - 2 : ny] = W[c, x + 1, ny - 2 : ny]
-                for p in range(parts):
-                    t = 2 + 4 * p
-                    nW[c, x - a, t : t + 4] = W[c, x + 1, t : t + 4] + C[c, x + 1, t : t + 4] * rL[x - a, p, c]
+                nW[c, x - a] = W[c, x + 1, u:ny]
+                nW[c, x - a, 2:6] = W[c, x + 1, u + 2 : u + 6] + C[c, x + 1, u + 2 : u + 6] * rL[x - a, 0, c]
         for x in range(a, nx - 1):
-            n1[x - a] = first_change(SC[x], S[x], w(0, x), w(0, x - 1), w(1, x), up_r[0, x], w(2, x))
+            n1[x - a] = first_change(
+                SC[x, u:ny], S[x, u:ny], w(0, x), w(0, x - 1), w(1, x), W[1, x + 1, u - 1 : u], w(2, x)
+            )
         for x in range(a - 1, nx):
             e = x + 1
             n2[x - (a - 1)] = second_change(
-                SC[x], change(x), change(x + 1), change(x - 1), c1[e, ny : ny + 1], up_r[1, x],
-                C[0, e], C[0, x], C[1, e], Ch[x], C[2, e],
+                SC[x, u:ny], change(x), change(x + 1), change(x - 1), c1[e, ny : ny + 1], c1[e, u - 1 : u],
+                C[0, e, u:ny], C[0, x, u:ny], C[1, e, u:ny], C[1, e, u - 1 : u], C[2, e, u:ny],
             )
         for x in range(ready, nx):
-            e = x + 1
             here = second(x)
-            nP[x - ready] = Pr[x] + here
+            nP[x - ready] = Pr[x, u:ny] + here
             fresh = final_velocity(
-                [w(c, x) for c in range(3)], [C[c, e] for c in range(3)], here, second(x + 1), c2e[x]
+                [w(c, x) for c in range(3)], [C[c, x + 1, u:ny] for c in range(3)], here, second(x + 1), c2e[x]
             )
             for c in range(3):
                 nV[c, x - ready] = fresh[c]
-        for copy in late:
-            copy.start()
-
-    for copy in early + late:
-        copy.wait()
+        for c in range(3):
+            pltpu.make_async_copy(nV.at[c], out_v.at[c, rest, top], sem.at[0]).start()
+        pltpu.make_async_copy(nP, out_p.at[rest, top], sem.at[1]).start()
+
+    pltpu.make_async_copy(moved, out_v, sem.at[0]).wait()
+    pltpu.make_async_copy(pressed, out_p, sem.at[1]).wait()
 
 
 def body(counts, velocity, pressure, forcing, source, viscosity):
     _, steps, nx, ny, nz = velocity.shape
-    assert steps == 1 and nx >= 8 and ny >= 8 and ny % 4 == 0
-    groups = [(0, 2), (nx - 2, nx), (2, 4)] + groups_of(4, nx - 4, 4) + [(nx - 4, nx - 2)]
+    assert steps == 1 and nx >= 12 and ny >= 16 and ny % 8 == 0
+    parts = (ny - 4) // 4
+    last = (nx - 4, nx - 2)
+    whole = [(0, 2), (nx - 2, nx), (2, 4)] + groups_of(4, nx - 4, 4)
+    groups = [(a, b, 0, parts) for a, b in whole] + [(*last, 0, parts - 1), (*last, parts - 1, parts)]
     detour = (1, 3, 2, 2) if counts[0] == 4 else None
-    last = groups[-1]
-    parts = (ny - 4) // 4
     vmem = lambda *shape: pltpu.VMEM(shape, jnp.float32)
     rows = lambda *lead: vmem(*lead, nx, 1, nz)
     any_space = pl.BlockSpec(memory_space=pl.ANY)
     on_chip = pl.BlockSpec(memory_space=pltpu.VMEM)
     kept = (
-        vmem(3, nx, ny, nz), vmem(nx, ny, nz), vmem(last[1] - last[0], parts, 3, 4, nz),
+        vmem(3, nx, ny, nz), vmem(nx, ny, nz), vmem(2, 1, 3, 4, nz),
         vmem(3, nx + 1, ny, nz), vmem(3, nx + 1, ny, nz), vmem(nx + 2, ny + 8, nz), vmem(nx + 1, ny, nz), rows(),
         vmem(nx, ny, nz), vmem(nx, ny, nz), vmem(nx + 1, ny, nz), rows(2), rows(),
     )
@@ -479,10 +525,10 @@
             vmem(3, nx, 4, nz), vmem(3, nx, 4, nz),
             vmem(nx, parts, 3, 4, nz), vmem(nx, parts, 3, 4, nz), vmem(2, parts, 3, 4, nz),
             rows(4), rows(4), rows(4), rows(4), vmem(4, nx + 1, 1, nz), rows(4),
-            vmem(ny, nz), vmem(ny, nz), rows(2), rows(2), rows(2), vmem(4 * nx * ny, nz),
+            vmem(ny, nz), vmem(ny, nz), rows(2), rows(2), rows(2), rows(), vmem(4 * nx * ny, nz),
             pltpu.SemaphoreType.DMA((3,)),
             pltpu.SemaphoreType.DMA((4,)),
-            pltpu.SemaphoreType.DMA((9 + len(groups),)),
+            pltpu.SemaphoreType.DMA((10 + len(groups),)),
         ],
         compiler_params=pltpu.CompilerParams(
             collective_id=0, has_side_effects=True, vmem_limit_bytes=40 << 20
@@ -498,8 +544,8 @@
         in_specs=[on_chip] * len(kept),
         out_specs=(any_space, any_space),
         scratch_shapes=[
-            vmem(3, 6, ny, nz), vmem(6, ny, nz), vmem(3, 2, ny, nz), vmem(3, ny, nz), vmem(5, ny, nz),
-            pltpu.SemaphoreType.DMA((8,)),
+            vmem(3, 6, 8, nz), vmem(6, 8, nz), vmem(3, 2, 8, nz), vmem(3, 8, nz), vmem(5, 8, nz),
+            pltpu.SemaphoreType.DMA((2,)),
         ],
         compiler_params=pltpu.CompilerParams(vmem_limit_bytes=2 << 20),
         name="settle",

time: 22 us -> 21.9 us (level)
  no operation moved by 1% of the time
where the time goes in v4:
time: 21.9 us; the launch traced here: 21.5 us
  Pallas kernels  20.9 us (95%)
  between operations  0.64 us (3%)
    pallas_call x1, Pallas kernels, body(): pl.pallas_call(functools.partial(kernel, *counts, groups, detour), out_sh...  19.9 us
    pallas_call x1, Pallas kernels, body(): pl.pallas_call(functools.partial(settle, last), out_shape=(jax.ShapeDtype...  1.03 us

profile of v4, /device:TPU:14, one launch (start us, length us, event | category | flops | bytes accessed | tf_op | source)
XLA Modules:
  0.0 21.5 jit_solution(14434485354762124822)
XLA Ops:
  0.6 19.9 %smoother.1 = (f32[3,16,16,256]{3,2,1,0:T(8,128)S(1)}, f32[16,16,256]{2,1,0:T(8,128)S(1)}, f32[2,1,3,4,256]{4,3,2,1,0:T(4,128)S(1)}, f32[3,17,16,256]{3,2,1,0:T(...) custom-call(f32[3,16,16,256]{3,2,1,0:T(8,128)} %bitcast.8, ...), custom_call_target="tpu_custom_call" | custom-call | tf_op jit(solution)/shard_map/smoother/pallas_call | solution.py:518
  20.5 1.0 %settle.1 = (f32[3,16,16,256]{3,2,1,0:T(8,128)}, f32[16,16,256]{2,1,0:T(8,128)}) custom-call(f32[3,16,16,256]{3,2,1,0:T(8,128)S(1)} %get-tuple-element.17.moved, f32[16,16,256]{2,1,0:T(8,128)S(1)} %get-tuple-element.18.pressed, f32[2,1,3,4,256]{4,3,2,1,0:T(4,128)S(1)} %get-tuple-element.19.rL, f32[3,17,16,256]{3,2,1,0:T(8,128)S(1)} %get-tuple-element.20.W, ...), custom_call_target="tpu_custom_call" | custom-call | tf_op jit(solution)/shard_map/settle/pallas_call | solution.py:538

commit v5 on v4

--- a/solution.py
+++ b/solution.py
@@ -122,73 +122,71 @@
     for a, n in ((0, half), (half, nx - half)):
         for c in range(3):
             fetch(vel.at[c, pl.ds(a, n)], V.at[c, pl.ds(1 + a, n)], 0)
+    greet("gx", xu)
+    greet("gx", xd)
+    for beside in (yu, yd):
+
+        @pl.when(jnp.logical_not(first_row) & (beside != 0))
+        def _():
+            greet("gy", beside)
+
+    def remote(send, recv, source, target, axis, index):
+        return pltpu.make_async_remote_copy(
+            src_ref=source, dst_ref=target, send_sem=send_sem.at[send], recv_sem=recv_sem.at[recv],
+            device_id={axis: index}, device_id_type=MESH,
+        )
+
+    vx_up = remote(0, 0, V.at[:, nx], V.at[:, 0], "gx", xu)
+    vx_dn = remote(0, 0, V.at[:, 1], V.at[:, nx + 1], "gx", xd)
+    px_dn = remote(0, 0, Pr.at[0], Pr.at[nx], "gx", xd)
+    nx_up = remote(0, 0, Nu.at[0, nx], Nu.at[0, 0], "gx", xu)
+    three, fourth = pl.ds(0, 3), pl.ds(3, 1)
+    ry_up = remote(0, 6, yu_s.at[three], yu_r.at[three], "gy", yu)
+    ry_dn = remote(0, 6, yd_s.at[three], yd_r.at[three], "gy", yd)
+    rz_up = remote(0, 6, yu_s.at[fourth], yu_r.at[fourth], "gy", yu)
+    rz_dn = remote(0, 6, yd_s.at[fourth], yd_r.at[fourth], "gy", yd)
+    fe_up = remote(0, 1, fe_s, fe_r, "gx", xu)
+    fx_up = remote(0, 2, W.at[0, nx], W.at[0, 0], "gx", xu)
+    cx_dn = remote(0, 3, c1.at[1], c1.at[nx + 1], "gx", xd)
+    cx_up = remote(0, 3, c1.at[nx], c1.at[0], "gx", xu)
+    m_dn = remote(0, 2, m_s, Ce, "gy", yd)
+    y_up = remote(0, 2, up_s, up_r, "gy", yu)
+    y_dn = remote(0, 2, dn_s, dn_r, "gy", yd)
+    ex_dn = remote(0, 4, c2.at[0], c2.at[nx], "gx", xd)
+    edge = remote(1, 5, sE, rE, "ta", t_next)
+    landing = [rI.at[pl.ds(a, b - a), pl.ds(p, q - p)] for a, b, p, q in groups[:final]] + [rL]
+    leaving = [sI.at[pl.ds(a, b - a), pl.ds(p, q - p)] for a, b, p, q in groups]
+    pieces = [remote(1, 7 + max(k, 1), leaving[k], landing[k], "ta", t_next) for k in range(final + 1)]
+    if detour:
+        to_via = remote(1, 7, leaving[lane], rR, "ta", via)
+        from_via = remote(1, 7 + lane, rR, landing[lane], "ta", taker)
+
+    def pack_edges(x):
+        for c in range(3):
+            sE[c, x, 0:2] = V[c, x + 1, 0:2]
+            sE[c, x, 2:4] = V[c, x + 1, ny - 2 : ny]
+
+    def pack_rows(x):
+        for c in range(3):
+            yu_s[c, x] = V[c, x + 1, ny - 1 : ny]
+            yd_s[c, x] = V[c, x + 1, 0:1]
+
+    def pack_more(x):
+        yu_s[3, x] = Nu[1, x + 1, ny - 1 : ny]
+        yd_s[3, x] = Pr[x, 0:1]
+
+    def pack_inner(x):
+        for c in range(3):
+            for p in range(parts):
+                sI[x, p, c] = V[c, x + 1, 2 + 4 * p : 6 + 4 * p]
+
+    wait_rows(load_sem.at[0], 3 * nx * ny)
     for c in range(3):
         fetch(vis.at[c], Nu.at[c, pl.ds(1, nx)], 1)
     fetch(prs, Pr.at[pl.ds(0, nx)], 1)
     for c in range(3):
         fetch(frc.at[c], F.at[c], 2)
     fetch(src, S, 2)
-
-    greet("gx", xu)
-    greet("gx", xd)
-    for beside in (yu, yd):
-
-        @pl.when(jnp.logical_not(first_row) & (beside != 0))
-        def _():
-            greet("gy", beside)
-
-    def remote(send, recv, source, target, axis, index):
-        return pltpu.make_async_remote_copy(
-            src_ref=source, dst_ref=target, send_sem=send_sem.at[send], recv_sem=recv_sem.at[recv],
-            device_id={axis: index}, device_id_type=MESH,
-        )
-
-    vx_up = remote(0, 0, V.at[:, nx], V.at[:, 0], "gx", xu)
-    vx_dn = remote(0, 0, V.at[:, 1], V.at[:, nx + 1], "gx", xd)
-    px_dn = remote(0, 0, Pr.at[0], Pr.at[nx], "gx", xd)
-    nx_up = remote(0, 0, Nu.at[0, nx], Nu.at[0, 0], "gx", xu)
-    three, fourth = pl.ds(0, 3), pl.ds(3, 1)
-    ry_up = remote(0, final + 9, yu_s.at[three], yu_r.at[three], "gy", yu)
-    ry_dn = remote(0, final + 9, yd_s.at[three], yd_r.at[three], "gy", yd)
-    rz_up = remote(0, final + 9, yu_s.at[fourth], yu_r.at[fourth], "gy", yu)
-    rz_dn = remote(0, final + 9, yd_s.at[fourth], yd_r.at[fourth], "gy", yd)
-    fe_up = remote(0, 1, fe_s, fe_r, "gx", xu)
-    fx_up = remote(0, 3, W.at[0, nx], W.at[0, 0], "gx", xu)
-    cx_dn = remote(0, 4, c1.at[1], c1.at[nx + 1], "gx", xd)
-    cx_up = remote(0, 4, c1.at[nx], c1.at[0], "gx", xu)
-    m_dn = remote(0, 2, m_s, Ce.at[:, pl.ds(1, nx)], "gy", yd)
-    ce_up = remote(3, 5, Ce.at[0, nx], Ce.at[0, 0], "gx", xu)
-    y_up = remote(0, 3, up_s, up_r, "gy", yu)
-    y_dn = remote(0, 3, dn_s, dn_r, "gy", yd)
-    ex_dn = remote(0, 6, c2.at[0], c2.at[nx], "gx", xd)
-    edge = remote(1, 7, sE, rE, "ta", t_next)
-    landing = [rI.at[pl.ds(a, b - a), pl.ds(p, q - p)] for a, b, p, q in groups[:final]] + [rL]
-    leaving = [sI.at[pl.ds(a, b - a), pl.ds(p, q - p)] for a, b, p, q in groups]
-    pieces = [remote(1, 8 + k, leaving[k], landing[k], "ta", t_next) for k in range(final + 1)]
-    if detour:
-        to_via = remote(1, 10 + final, leaving[lane], rR, "ta", via)
-        from_via = remote(2, 8 + lane, rR, landing[lane], "ta", taker)
-
-    def pack_edges(x):
-        for c in range(3):
-            sE[c, x, 0:2] = V[c, x + 1, 0:2]
-            sE[c, x, 2:4] = V[c, x + 1, ny - 2 : ny]
-
-    def pack_rows(x):
-        for c in range(3):
-            yu_s[c, x] = V[c, x + 1, ny - 1 : ny]
-            yd_s[c, x] = V[c, x + 1, 0:1]
-
-    def pack_more(x):
-        yu_s[3, x] = Nu[1, x + 1, ny - 1 : ny]
-        yd_s[3, x] = Pr[x, 0:1]
-
-    def pack_inner(x):
-        for c in range(3):
-            for p in range(parts):
-                sI[x, p, c] = V[c, x + 1, 2 + 4 * p : 6 + 4 * p]
-
-    wait_rows(load_sem.at[0], 3 * nx * ny)
     loop(0, nx, pack_edges)
     pl.semaphore_wait(barrier, expected)
 
@@ -223,9 +221,11 @@
 
     loop(0, nx, pack_inner)
 
-    @pl.when(has_next)
-    def _():
-        for k, copy in enumerate(pieces):
+    pauses = first_row & (ta == 0) & (lax.rem(gx, 2) == 1)
+    outer_rows = 12 * nx + 48 * parts
+
+    def send_inner():
+        for k in range(2, final + 1):
             if detour and k == lane:
 
                 @pl.when(ta == giver)
@@ -234,10 +234,19 @@
 
                 @pl.when(ta != giver)
                 def _():
-                    copy.start()
+                    pieces[k].start()
 
             else:
-                copy.start()
+                pieces[k].start()
+
+    @pl.when(has_next)
+    def _():
+        pieces[0].start()
+        pieces[1].start()
+
+    @pl.when(has_next & jnp.logical_not(pauses))
+    def _():
+        send_inner()
 
     @pl.when(first_row)
     def _():
@@ -282,7 +291,7 @@
 
     loop(0, nx, prepare)
     m_dn.start()
-    wait_rows(recv_sem.at[final + 9], 8 * nx)
+    wait_rows(recv_sem.at[6], 8 * nx)
     loop(0, nx, complete)
     if detour:
 
@@ -304,17 +313,17 @@
                 t = 2 + 4 * p
                 W[c, x + 1, t : t + 4] = W[c, x + 1, t : t + 4] + C[c, x + 1, t : t + 4] * rI[x, p, c]
 
+    @pl.when(has_prev)
+    def _():
+        edge.wait_recv()
+        loop(0, nx, add_edges)
+
     def arrive(k):
         @pl.when(has_prev)
         def _():
             pieces[k].wait_recv()
             a, b, p, q = groups[k]
             loop(a, b, lambda x: add_inner(x, p, q))
-
-    @pl.when(has_prev)
-    def _():
-        edge.wait_recv()
-        loop(0, nx, add_edges)
 
     fe_s[...] = W[0, nx]
     fe_up.start()
@@ -334,12 +343,19 @@
     y_up.start()
     y_dn.start()
 
-    arrive(0)
-    arrive(1)
+    @pl.when(has_next & pauses)
+    def _():
+        wait_rows(send_sem.at[1], outer_rows)
+        send_inner()
+
+    @pl.when(has_prev)
+    def _():
+        wait_rows(recv_sem.at[8], 48 * parts)
+        for a in (0, nx - 2):
+            loop(a, a + 2, lambda x: add_inner(x, 0, parts))
+
     fx_up.start()
-    m_dn.wait_recv()
-    ce_up.start()
-    wait_rows(recv_sem.at[3], ny + 4 * nx)
+    wait_rows(recv_sem.at[2], ny + 8 * nx)
 
     def first(x):
         e = x + 1
@@ -347,19 +363,19 @@
 
     def first_above(x):
         e = x + 1
-        scale = damping / (Ce[3, e] + C[1, e, ny - 1 : ny])
+        scale = damping / (Ce[3, x] + C[1, e, ny - 1 : ny])
         Se[x] = scale
         c1[e, ny : ny + 1] = dn_r[0, x] + scale * W[1, e, ny - 1 : ny]
 
     for x in (0, nx - 1):
         first(x)
         first_above(x)
+    c1[nx, ny + 1 : ny + 2] = Ce[0, nx - 1]
     for copy in (cx_dn, cx_up):
         copy.start()
     loop(1, nx - 1, first)
     loop(1, nx - 1, first_above)
-    wait_rows(recv_sem.at[4], 2 * (ny + 8))
-    ce_up.wait_recv()
+    wait_rows(recv_sem.at[3], 2 * (ny + 8))
 
     def second(x):
         e = x + 1
@@ -368,21 +384,22 @@
             C[0, e], C[0, x], C[1, e], Ch[x], C[2, e],
         )
 
-    def second_above(x):
+    def second_above(x, c0_last):
         e = x + 1
         wide = lambda row: jnp.broadcast_to(row, (8, nz))
         here = wide(c1[e, ny : ny + 1])
-        g0 = wide(Ce[0, e]) * (wide(c1[e + 1, ny : ny + 1]) - here)
-        g0_last = wide(Ce[0, x]) * (here - wide(c1[e - 1, ny : ny + 1]))
-        g1 = wide(Ce[1, e]) * (wide(dn_r[1, x]) - here)
+        g0 = wide(Ce[0, x]) * (wide(c1[e + 1, ny : ny + 1]) - here)
+        g0_last = wide(c0_last) * (here - wide(c1[e - 1, ny : ny + 1]))
+        g1 = wide(Ce[1, x]) * (wide(dn_r[1, x]) - here)
         g1_last = wide(C[1, e, ny - 1 : ny]) * (here - wide(c1[e, ny - 1 : ny]))
-        g2 = wide(Ce[2, e]) * (z_next(here) - here)
+        g2 = wide(Ce[2, x]) * (z_next(here) - here)
         div = (g0 - g0_last) + (g1 - g1_last) + (g2 - z_last(g2))
         c2e[x] = (2.0 * here + wide(Se[x]) * div)[0:1]
 
     second(0)
     ex_dn.start()
-    loop(0, nx, second_above)
+    second_above(0, c1[0, ny + 1 : ny + 2])
+    loop(1, nx, lambda x: second_above(x, Ce[0, x - 1]))
 
     def finish(x):
         e = x + 1
@@ -427,24 +444,28 @@
     def _():
         pieces[final].wait_recv()
 
-    @pl.when(has_next)
+    @pl.when(has_next & jnp.logical_not(pauses))
     def _():
         wait_rows(send_sem.at[1], 3 * nx * ny)
 
+    @pl.when(has_next & pauses)
+    def _():
+        wait_rows(send_sem.at[1], 3 * nx * ny - outer_rows)
+
     if detour:
 
         @pl.when(ta == via)
         def _():
-            from_via.wait_send()
-
-    ce_up.wait_send()
+            wait_rows(send_sem.at[1], 24 * parts)
+
     wait_rows(send_sem.at[0], 13 * ny + 16 + 16 * nx)
 
 
 def settle(
-    last, moved, pressed, rL, W, C, c1, c2, c2e, SC, S, Pr, up_r, Ch, out_v, out_p, nV, nP, nW, n1, n2, sem
+    last, moved, pressed, rL, W, C, c1, c2, c2e, SC, S, Pr, up_r, Ch, step_v, step_p, nV, nP, nW, n1, n2, sem
 ):
-    _, nx, ny, nz = out_v.shape
+    out_v, out_p = step_v.at[:, 0], step_p.at[0]
+    _, nx, ny, nz = moved.shape
     a, b = last
     ready, u = a - 2, ny - 8
     done, rest = pl.ds(0, ready), pl.ds(ready, nx - ready)
@@ -524,22 +545,22 @@
             vmem(3, nx + 2, ny, nz), vmem(3, nx, ny, nz), vmem(3, nx + 1, ny, nz),
             vmem(3, nx, 4, nz), vmem(3, nx, 4, nz),
             vmem(nx, parts, 3, 4, nz), vmem(nx, parts, 3, 4, nz), vmem(2, parts, 3, 4, nz),
-            rows(4), rows(4), rows(4), rows(4), vmem(4, nx + 1, 1, nz), rows(4),
+            rows(4), rows(4), rows(4), rows(4), rows(4), rows(4),
             vmem(ny, nz), vmem(ny, nz), rows(2), rows(2), rows(2), rows(), vmem(4 * nx * ny, nz),
             pltpu.SemaphoreType.DMA((3,)),
-            pltpu.SemaphoreType.DMA((4,)),
-            pltpu.SemaphoreType.DMA((10 + len(groups),)),
+            pltpu.SemaphoreType.DMA((2,)),
+            pltpu.SemaphoreType.DMA((7 + len(groups),)),
         ],
         compiler_params=pltpu.CompilerParams(
             collective_id=0, has_side_effects=True, vmem_limit_bytes=40 << 20
         ),
         name="smoother",
     )(*(pltpu.with_memory_space_constraint(a, pltpu.HBM) for a in inputs))
-    out_v, out_p = pl.pallas_call(
+    return pl.pallas_call(
         functools.partial(settle, last),
         out_shape=(
-            jax.ShapeDtypeStruct((3, nx, ny, nz), jnp.float32),
-            jax.ShapeDtypeStruct((nx, ny, nz), jnp.float32),
+            jax.ShapeDtypeStruct((3, 1, nx, ny, nz), jnp.float32),
+            jax.ShapeDtypeStruct((1, nx, ny, nz), jnp.float32),
         ),
         in_specs=[on_chip] * len(kept),
         out_specs=(any_space, any_space),
@@ -550,7 +571,6 @@
         compiler_params=pltpu.CompilerParams(vmem_limit_bytes=2 << 20),
         name="settle",
     )(*held)
-    return out_v[:, None], out_p[None]
 
 
 def solution(mesh):

time: 21.9 us -> 21.6 us (0.986); the launches traced: 21.5 us -> 21.5 us
  no operation moved by 1% of the time
where the time goes in v5:
time: 21.6 us; the launch traced here: 21.5 us
  Pallas kernels  20.9 us (97%)
  between operations  0.64 us (3%)
    pallas_call x1, Pallas kernels, body(): pl.pallas_call(functools.partial(kernel, *counts, groups, detour), out_sh...  19.8 us
    pallas_call x1, Pallas kernels, body(): pl.pallas_call(functools.partial(settle, last), out_shape=(jax.ShapeDtype...  1.03 us

profile of v5, /device:TPU:14, one launch (start us, length us, event | category | flops | bytes accessed | tf_op | source)
XLA Modules:
  0.0 21.5 jit_solution(5051655035199581492)
XLA Ops:
  0.6 19.8 %smoother.1 = (f32[3,16,16,256]{3,2,1,0:T(8,128)S(1)}, f32[16,16,256]{2,1,0:T(8,128)S(1)}, f32[2,1,3,4,256]{4,3,2,1,0:T(4,128)S(1)}, f32[3,17,16,256]{3,2,1,0:T(...) custom-call(f32[3,16,16,256]{3,2,1,0:T(8,128)} %bitcast.4, ...), custom_call_target="tpu_custom_call" | custom-call | tf_op jit(solution)/shard_map/smoother/pallas_call | solution.py:539
  20.5 1.0 %settle.1 = (f32[3,1,16,16,256]{4,3,2,1,0:T(8,128)}, f32[1,16,16,256]{3,2,1,0:T(8,128)}) custom-call(f32[3,16,16,256]{3,2,1,0:T(8,128)S(1)} %get-tuple-element.15.moved, f32[16,16,256]{2,1,0:T(8,128)S(1)} %get-tuple-element.16.pressed, f32[2,1,3,4,256]{4,3,2,1,0:T(4,128)S(1)} %get-tuple-element.17.rL, f32[3,17,16,256]{3,2,1,0:T(8,128)S(1)} %get-tuple-element.18.W, ...), custom_call_target="tpu_custom_call" | custom-call | tf_op jit(solution)/shard_map/settle/pallas_call | solution.py:559

commit v6 on v5

--- a/solution.py
+++ b/solution.py
@@ -185,8 +185,8 @@
         fetch(vis.at[c], Nu.at[c, pl.ds(1, nx)], 1)
     fetch(prs, Pr.at[pl.ds(0, nx)], 1)
     for c in range(3):
-        fetch(frc.at[c], F.at[c], 2)
-    fetch(src, S, 2)
+        fetch(frc.at[c], F.at[c], 1)
+    fetch(src, S, 1)
     loop(0, nx, pack_edges)
     pl.semaphore_wait(barrier, expected)
 
@@ -209,7 +209,7 @@
         ry_up.start()
         ry_dn.start()
 
-    wait_rows(load_sem.at[1], 4 * nx * ny)
+    wait_rows(load_sem.at[1], 8 * nx * ny)
     loop(0, nx, pack_more)
     for copy in (px_dn, nx_up):
         copy.start()
@@ -254,7 +254,6 @@
         for copy in (ry_up, ry_dn, rz_up, rz_dn):
             copy.start()
 
-    wait_rows(load_sem.at[2], 4 * nx * ny)
     wait_rows(recv_sem.at[0], 8 * ny)
     C[0, 0] = coeff_of(Nu[0, 0])
 
@@ -411,16 +410,24 @@
         for c in range(3):
             OV[c, x] = moved[c]
 
-    def finish_low(x):
-        e, low = x + 1, slice(0, ny - 8)
-        here = c2[x, low]
-        OP[x, low] = Pr[x, low] + here
+    top = slice(8, ny)
+
+    def second_top(x):
+        e = x + 1
+        c2[x, top] = second_change(
+            SC[x, top], c1[e, top], c1[e + 1, top], c1[e - 1, top], c1[e, ny : ny + 1], c1[e, 7:8],
+            C[0, e, top], C[0, x, top], C[1, e, top], C[1, e, 7:8], C[2, e, top],
+        )
+
+    def finish_top(x):
+        e = x + 1
+        here = c2[x, top]
+        OP[x, top] = Pr[x, top] + here
         moved = final_velocity(
-            [W[c, e, low] for c in range(3)], [C[c, e, low] for c in range(3)], here, c2[x + 1, low],
-            c2[x, ny - 8 : ny - 7],
+            [W[c, e, top] for c in range(3)], [C[c, e, top] for c in range(3)], here, c2[x + 1, top], c2e[x]
         )
         for c in range(3):
-            OV[c, x, low] = moved[c]
+            OV[c, x, top] = moved[c]
 
     for k in range(2, final - 1):
         a, b, _, _ = groups[k]
@@ -437,8 +444,8 @@
     a = groups[final][0]
     arrive(final - 1)
     loop(a, nx - 1, first)
-    loop(a - 1, nx, second)
-    loop(a - 2, nx, finish_low)
+    loop(a - 1, nx, second_top)
+    loop(a - 2, nx, finish_top)
 
     @pl.when(has_prev)
     def _():
@@ -467,52 +474,50 @@
     out_v, out_p = step_v.at[:, 0], step_p.at[0]
     _, nx, ny, nz = moved.shape
     a, b = last
-    ready, u = a - 2, ny - 8
+    ready, low = a - 2, slice(0, 8)
     done, rest = pl.ds(0, ready), pl.ds(ready, nx - ready)
-    low, top = pl.ds(0, u), pl.ds(u, 8)
+    bottom, top = pl.ds(0, 8), pl.ds(8, ny - 8)
 
     for c in range(3):
         pltpu.make_async_copy(moved.at[c, done], out_v.at[c, done], sem.at[0]).start()
-        pltpu.make_async_copy(moved.at[c, rest, low], out_v.at[c, rest, low], sem.at[0]).start()
+        pltpu.make_async_copy(moved.at[c, rest, top], out_v.at[c, rest, top], sem.at[0]).start()
     pltpu.make_async_copy(pressed.at[done], out_p.at[done], sem.at[1]).start()
-    pltpu.make_async_copy(pressed.at[rest, low], out_p.at[rest, low], sem.at[1]).start()
+    pltpu.make_async_copy(pressed.at[rest, top], out_p.at[rest, top], sem.at[1]).start()
 
     def w(c, x):
-        return nW[c, x - a] if a <= x < b else W[c, x + 1, u:ny]
+        return nW[c, x - a] if a <= x < b else W[c, x + 1, low]
 
     def change(x):
-        return n1[x - a] if a <= x < nx - 1 else c1[x + 1, u:ny]
+        return n1[x - a] if a <= x < nx - 1 else c1[x + 1, low]
 
     def second(x):
-        return n2[x - (a - 1)] if a - 1 <= x < nx else c2[x, u:ny]
+        return n2[x - (a - 1)] if a - 1 <= x < nx else c2[x, low]
 
     @pl.when(lax.axis_index("ta") >= 0)
     def _():
         for x in range(a, b):
             for c in range(3):
-                nW[c, x - a] = W[c, x + 1, u:ny]
-                nW[c, x - a, 2:6] = W[c, x + 1, u + 2 : u + 6] + C[c, x + 1, u + 2 : u + 6] * rL[x - a, 0, c]
+                nW[c, x - a] = W[c, x + 1, low]
+                nW[c, x - a, 2:6] = W[c, x + 1, 2:6] + C[c, x + 1, 2:6] * rL[x - a, 0, c]
         for x in range(a, nx - 1):
-            n1[x - a] = first_change(
-                SC[x, u:ny], S[x, u:ny], w(0, x), w(0, x - 1), w(1, x), W[1, x + 1, u - 1 : u], w(2, x)
-            )
+            n1[x - a] = first_change(SC[x, low], S[x, low], w(0, x), w(0, x - 1), w(1, x), up_r[0, x], w(2, x))
         for x in range(a - 1, nx):
             e = x + 1
             n2[x - (a - 1)] = second_change(
-                SC[x, u:ny], change(x), change(x + 1), change(x - 1), c1[e, ny : ny + 1], c1[e, u - 1 : u],
-                C[0, e, u:ny], C[0, x, u:ny], C[1, e, u:ny], C[1, e, u - 1 : u], C[2, e, u:ny],
+                SC[x, low], change(x), change(x + 1), change(x - 1), c1[e, 8:9], up_r[1, x],
+                C[0, e, low], C[0, x, low], C[1, e, low], Ch[x], C[2, e, low],
             )
         for x in range(ready, nx):
             here = second(x)
-            nP[x - ready] = Pr[x, u:ny] + here
+            nP[x - ready] = Pr[x, low] + here
             fresh = final_velocity(
-                [w(c, x) for c in range(3)], [C[c, x + 1, u:ny] for c in range(3)], here, second(x + 1), c2e[x]
+                [w(c, x) for c in range(3)], [C[c, x + 1, low] for c in range(3)], here, second(x + 1), c2[x, 8:9]
             )
             for c in range(3):
                 nV[c, x - ready] = fresh[c]
         for c in range(3):
-            pltpu.make_async_copy(nV.at[c], out_v.at[c, rest, top], sem.at[0]).start()
-        pltpu.make_async_copy(nP, out_p.at[rest, top], sem.at[1]).start()
+            pltpu.make_async_copy(nV.at[c], out_v.at[c, rest, bottom], sem.at[0]).start()
+        pltpu.make_async_copy(nP, out_p.at[rest, bottom], sem.at[1]).start()
 
     pltpu.make_async_copy(moved, out_v, sem.at[0]).wait()
     pltpu.make_async_copy(pressed, out_p, sem.at[1]).wait()
@@ -524,7 +529,7 @@
     parts = (ny - 4) // 4
     last = (nx - 4, nx - 2)
     whole = [(0, 2), (nx - 2, nx), (2, 4)] + groups_of(4, nx - 4, 4)
-    groups = [(a, b, 0, parts) for a, b in whole] + [(*last, 0, parts - 1), (*last, parts - 1, parts)]
+    groups = [(a, b, 0, parts) for a, b in whole] + [(*last, 1, parts), (*last, 0, 1)]
     detour = (1, 3, 2, 2) if counts[0] == 4 else None
     vmem = lambda *shape: pltpu.VMEM(shape, jnp.float32)
     rows = lambda *lead: vmem(*lead, nx, 1, nz)
@@ -546,8 +551,8 @@
             vmem(3, nx, 4, nz), vmem(3, nx, 4, nz),
             vmem(nx, parts, 3, 4, nz), vmem(nx, parts, 3, 4, nz), vmem(2, parts, 3, 4, nz),
             rows(4), rows(4), rows(4), rows(4), rows(4), rows(4),
-            vmem(ny, nz), vmem(ny, nz), rows(2), rows(2), rows(2), rows(), vmem(4 * nx * ny, nz),
-            pltpu.SemaphoreType.DMA((3,)),
+            vmem(ny, nz), vmem(ny, nz), rows(2), rows(2), rows(2), rows(), vmem(8 * nx * ny, nz),
+            pltpu.SemaphoreType.DMA((2,)),
             pltpu.SemaphoreType.DMA((2,)),
             pltpu.SemaphoreType.DMA((7 + len(groups),)),
         ],

time: 21.6 us -> 21.6 us (level)
  no operation moved by 1% of the time
where the time goes in v6:
time: 21.6 us; the launch traced here: 21.5 us
  Pallas kernels  20.9 us (97%)
  between operations  0.64 us (3%)
    pallas_call x1, Pallas kernels, body(): pl.pallas_call(functools.partial(kernel, *counts, groups, detour), out_sh...  19.8 us
    pallas_call x1, Pallas kernels, body(): pl.pallas_call(functools.partial(settle, last), out_shape=(jax.ShapeDtype...  1.03 us

profile of v6, /device:TPU:14, one launch (start us, length us, event | category | flops | bytes accessed | tf_op | source)
XLA Modules:
  0.0 21.5 jit_solution(174914272337680046)
XLA Ops:
  0.6 19.8 %smoother.1 = (f32[3,16,16,256]{3,2,1,0:T(8,128)S(1)}, f32[16,16,256]{2,1,0:T(8,128)S(1)}, f32[2,1,3,4,256]{4,3,2,1,0:T(4,128)S(1)}, f32[3,17,16,256]{3,2,1,0:T(...) custom-call(f32[3,16,16,256]{3,2,1,0:T(8,128)} %bitcast.4, ...), custom_call_target="tpu_custom_call" | custom-call | tf_op jit(solution)/shard_map/smoother/pallas_call | solution.py:544
  20.5 1.0 %settle.1 = (f32[3,1,16,16,256]{4,3,2,1,0:T(8,128)}, f32[1,16,16,256]{3,2,1,0:T(8,128)}) custom-call(f32[3,16,16,256]{3,2,1,0:T(8,128)S(1)} %get-tuple-element.15.moved, f32[16,16,256]{2,1,0:T(8,128)S(1)} %get-tuple-element.16.pressed, f32[2,1,3,4,256]{4,3,2,1,0:T(4,128)S(1)} %get-tuple-element.17.rL, f32[3,17,16,256]{3,2,1,0:T(8,128)S(1)} %get-tuple-element.18.W, ...), custom_call_target="tpu_custom_call" | custom-call | tf_op jit(solution)/shard_map/settle/pallas_call | solution.py:564

commit v7 on v6

--- a/solution.py
+++ b/solution.py
@@ -185,8 +185,8 @@
         fetch(vis.at[c], Nu.at[c, pl.ds(1, nx)], 1)
     fetch(prs, Pr.at[pl.ds(0, nx)], 1)
     for c in range(3):
-        fetch(frc.at[c], F.at[c], 1)
-    fetch(src, S, 1)
+        fetch(frc.at[c], F.at[c], 2)
+    fetch(src, S, 2)
     loop(0, nx, pack_edges)
     pl.semaphore_wait(barrier, expected)
 
@@ -209,7 +209,7 @@
         ry_up.start()
         ry_dn.start()
 
-    wait_rows(load_sem.at[1], 8 * nx * ny)
+    wait_rows(load_sem.at[1], 4 * nx * ny)
     loop(0, nx, pack_more)
     for copy in (px_dn, nx_up):
         copy.start()
@@ -254,6 +254,7 @@
         for copy in (ry_up, ry_dn, rz_up, rz_dn):
             copy.start()
 
+    wait_rows(load_sem.at[2], 4 * nx * ny)
     wait_rows(recv_sem.at[0], 8 * ny)
     C[0, 0] = coeff_of(Nu[0, 0])
 
@@ -551,8 +552,8 @@
             vmem(3, nx, 4, nz), vmem(3, nx, 4, nz),
             vmem(nx, parts, 3, 4, nz), vmem(nx, parts, 3, 4, nz), vmem(2, parts, 3, 4, nz),
             rows(4), rows(4), rows(4), rows(4), rows(4), rows(4),
-            vmem(ny, nz), vmem(ny, nz), rows(2), rows(2), rows(2), rows(), vmem(8 * nx * ny, nz),
-            pltpu.SemaphoreType.DMA((2,)),
+            vmem(ny, nz), vmem(ny, nz), rows(2), rows(2), rows(2), rows(), vmem(4 * nx * ny, nz),
+            pltpu.SemaphoreType.DMA((3,)),
             pltpu.SemaphoreType.DMA((2,)),
             pltpu.SemaphoreType.DMA((7 + len(groups),)),
         ],

time: 21.6 us -> 21.6 us (level)
  no operation moved by 1% of the time
where the time goes in v7:
time: 21.6 us; the launch traced here: 21.5 us
  Pallas kernels  20.9 us (97%)
  between operations  0.64 us (3%)
    pallas_call x1, Pallas kernels, body(): pl.pallas_call(functools.partial(kernel, *counts, groups, detour), out_sh...  19.8 us
    pallas_call x1, Pallas kernels, body(): pl.pallas_call(functools.partial(settle, last), out_shape=(jax.ShapeDtype...  1.03 us

profile of v7, /device:TPU:14, one launch (start us, length us, event | category | flops | bytes accessed | tf_op | source)
XLA Modules:
  0.0 21.5 jit_solution(16769965640186970615)
XLA Ops:
  0.6 19.8 %smoother.1 = (f32[3,16,16,256]{3,2,1,0:T(8,128)S(1)}, f32[16,16,256]{2,1,0:T(8,128)S(1)}, f32[2,1,3,4,256]{4,3,2,1,0:T(4,128)S(1)}, f32[3,17,16,256]{3,2,1,0:T(...) custom-call(f32[3,16,16,256]{3,2,1,0:T(8,128)} %bitcast.4, ...), custom_call_target="tpu_custom_call" | custom-call | tf_op jit(solution)/shard_map/smoother/pallas_call | solution.py:545
  20.5 1.0 %settle.1 = (f32[3,1,16,16,256]{4,3,2,1,0:T(8,128)}, f32[1,16,16,256]{3,2,1,0:T(8,128)}) custom-call(f32[3,16,16,256]{3,2,1,0:T(8,128)S(1)} %get-tuple-element.15.moved, f32[16,16,256]{2,1,0:T(8,128)S(1)} %get-tuple-element.16.pressed, f32[2,1,3,4,256]{4,3,2,1,0:T(4,128)S(1)} %get-tuple-element.17.rL, f32[3,17,16,256]{3,2,1,0:T(8,128)S(1)} %get-tuple-element.18.W, ...), custom_call_target="tpu_custom_call" | custom-call | tf_op jit(solution)/shard_map/settle/pallas_call | solution.py:565

commit v8 on v7

--- a/solution.py
+++ b/solution.py
@@ -529,7 +529,7 @@
     assert steps == 1 and nx >= 12 and ny >= 16 and ny % 8 == 0
     parts = (ny - 4) // 4
     last = (nx - 4, nx - 2)
-    whole = [(0, 2), (nx - 2, nx), (2, 4)] + groups_of(4, nx - 4, 4)
+    whole = [(0, 2), (nx - 2, nx), (2, 4)] + groups_of(4, nx - 6, 4) + [(nx - 6, nx - 4)]
     groups = [(a, b, 0, parts) for a, b in whole] + [(*last, 1, parts), (*last, 0, 1)]
     detour = (1, 3, 2, 2) if counts[0] == 4 else None
     vmem = lambda *shape: pltpu.VMEM(shape, jnp.float32)

time: 21.6 us -> 21.7 us (level)
  no operation moved by 1% of the time
where the time goes in v8:
time: 21.7 us; the launch traced here: 21.5 us
  Pallas kernels  20.9 us (96%)
  between operations  0.64 us (3%)
    pallas_call x1, Pallas kernels, body(): pl.pallas_call(functools.partial(kernel, *counts, groups, detour), out_sh...  19.8 us
    pallas_call x1, Pallas kernels, body(): pl.pallas_call(functools.partial(settle, last), out_shape=(jax.ShapeDtype...  1.03 us

profile of v8, /device:TPU:14, one launch (start us, length us, event | category | flops | bytes accessed | tf_op | source)
XLA Modules:
  0.0 21.5 jit_solution(16734093072970981799)
XLA Ops:
  0.6 19.8 %smoother.1 = (f32[3,16,16,256]{3,2,1,0:T(8,128)S(1)}, f32[16,16,256]{2,1,0:T(8,128)S(1)}, f32[2,1,3,4,256]{4,3,2,1,0:T(4,128)S(1)}, f32[3,17,16,256]{3,2,1,0:T(...) custom-call(f32[3,16,16,256]{3,2,1,0:T(8,128)} %bitcast.4, ...), custom_call_target="tpu_custom_call" | custom-call | tf_op jit(solution)/shard_map/smoother/pallas_call | solution.py:545
  20.5 1.0 %settle.1 = (f32[3,1,16,16,256]{4,3,2,1,0:T(8,128)}, f32[1,16,16,256]{3,2,1,0:T(8,128)}) custom-call(f32[3,16,16,256]{3,2,1,0:T(8,128)S(1)} %get-tuple-element.15.moved, f32[16,16,256]{2,1,0:T(8,128)S(1)} %get-tuple-element.16.pressed, f32[2,1,3,4,256]{4,3,2,1,0:T(4,128)S(1)} %get-tuple-element.17.rL, f32[3,17,16,256]{3,2,1,0:T(8,128)S(1)} %get-tuple-element.18.W, ...), custom_call_target="tpu_custom_call" | custom-call | tf_op jit(solution)/shard_map/settle/pallas_call | solution.py:565

commit v9 on v7

--- a/solution.py
+++ b/solution.py
@@ -82,7 +82,7 @@
     parts = (ny - 4) // 4
     final = len(groups) - 1
     ta, gx, gy = lax.axis_index("ta"), lax.axis_index("gx"), lax.axis_index("gy")
-    t_next, t_prev = lax.rem(ta + 1, slabs), lax.rem(ta + slabs - 1, slabs)
+    t_next = jnp.minimum(ta + 1, slabs - 1)
     has_next, has_prev = ta < slabs - 1, ta > 0
     xu, xd = lax.rem(gx + 1, nx_parts), lax.rem(gx + nx_parts - 1, nx_parts)
     yu, yd = lax.rem(gy + 1, ny_parts), lax.rem(gy + ny_parts - 1, ny_parts)
@@ -95,7 +95,7 @@
 
     @pl.when(has_prev)
     def _():
-        greet("ta", t_prev)
+        greet("ta", ta - 1)
 
     expected = 2 + has_next.astype(jnp.int32) + jnp.where(first_row, 0, 2)
     if detour:

time: 21.6 us -> 21.6 us (level)
  no operation moved by 1% of the time
where the time goes in v9:
time: 21.6 us; the launch traced here: 21.5 us
  Pallas kernels  20.9 us (97%)
  between operations  0.64 us (3%)
    pallas_call x1, Pallas kernels, body(): pl.pallas_call(functools.partial(kernel, *counts, groups, detour), out_sh...  19.8 us
    pallas_call x1, Pallas kernels, body(): pl.pallas_call(functools.partial(settle, last), out_shape=(jax.ShapeDtype...  1.03 us

profile of v9, /device:TPU:14, one launch (start us, length us, event | category | flops | bytes accessed | tf_op | source)
XLA Modules:
  0.0 21.5 jit_solution(6997290279333695655)
XLA Ops:
  0.6 19.8 %smoother.1 = (f32[3,16,16,256]{3,2,1,0:T(8,128)S(1)}, f32[16,16,256]{2,1,0:T(8,128)S(1)}, f32[2,1,3,4,256]{4,3,2,1,0:T(4,128)S(1)}, f32[3,17,16,256]{3,2,1,0:T(...) custom-call(f32[3,16,16,256]{3,2,1,0:T(8,128)} %bitcast.4, ...), custom_call_target="tpu_custom_call" | custom-call | tf_op jit(solution)/shard_map/smoother/pallas_call | solution.py:545
  20.5 1.0 %settle.1 = (f32[3,1,16,16,256]{4,3,2,1,0:T(8,128)}, f32[1,16,16,256]{3,2,1,0:T(8,128)}) custom-call(f32[3,16,16,256]{3,2,1,0:T(8,128)S(1)} %get-tuple-element.15.moved, f32[16,16,256]{2,1,0:T(8,128)S(1)} %get-tuple-element.16.pressed, f32[2,1,3,4,256]{4,3,2,1,0:T(4,128)S(1)} %get-tuple-element.17.rL, f32[3,17,16,256]{3,2,1,0:T(8,128)S(1)} %get-tuple-element.18.W, ...), custom_call_target="tpu_custom_call" | custom-call | tf_op jit(solution)/shard_map/settle/pallas_call | solution.py:565

commit v10 on v9

--- a/solution.py
+++ b/solution.py
@@ -517,8 +517,8 @@
             for c in range(3):
                 nV[c, x - ready] = fresh[c]
         for c in range(3):
-            pltpu.make_async_copy(nV.at[c], out_v.at[c, rest, bottom], sem.at[0]).start()
-        pltpu.make_async_copy(nP, out_p.at[rest, bottom], sem.at[1]).start()
+            pltpu.make_async_copy(nV.at[c], out_v.at[c, rest, bottom], sem.at[0]).start(priority=1)
+        pltpu.make_async_copy(nP, out_p.at[rest, bottom], sem.at[1]).start(priority=1)
 
     pltpu.make_async_copy(moved, out_v, sem.at[0]).wait()
     pltpu.make_async_copy(pressed, out_p, sem.at[1]).wait()

time: 21.6 us -> 21.6 us (level)
  no operation moved by 1% of the time
where the time goes in v10:
time: 21.6 us; the launch traced here: 21.5 us
  Pallas kernels  20.9 us (97%)
  between operations  0.64 us (3%)
    pallas_call x1, Pallas kernels, body(): pl.pallas_call(functools.partial(kernel, *counts, groups, detour), out_sh...  19.8 us
    pallas_call x1, Pallas kernels, body(): pl.pallas_call(functools.partial(settle, last), out_shape=(jax.ShapeDtype...  1.03 us

profile of v10, /device:TPU:14, one launch (start us, length us, event | category | flops | bytes accessed | tf_op | source)
XLA Modules:
  0.0 21.5 jit_solution(2580636602329044024)
XLA Ops:
  0.6 19.8 %smoother.1 = (f32[3,16,16,256]{3,2,1,0:T(8,128)S(1)}, f32[16,16,256]{2,1,0:T(8,128)S(1)}, f32[2,1,3,4,256]{4,3,2,1,0:T(4,128)S(1)}, f32[3,17,16,256]{3,2,1,0:T(...) custom-call(f32[3,16,16,256]{3,2,1,0:T(8,128)} %bitcast.4, ...), custom_call_target="tpu_custom_call" | custom-call | tf_op jit(solution)/shard_map/smoother/pallas_call | solution.py:545
  20.5 1.0 %settle.1 = (f32[3,1,16,16,256]{4,3,2,1,0:T(8,128)}, f32[1,16,16,256]{3,2,1,0:T(8,128)}) custom-call(f32[3,16,16,256]{3,2,1,0:T(8,128)S(1)} %get-tuple-element.15.moved, f32[16,16,256]{2,1,0:T(8,128)S(1)} %get-tuple-element.16.pressed, f32[2,1,3,4,256]{4,3,2,1,0:T(4,128)S(1)} %get-tuple-element.17.rL, f32[3,17,16,256]{3,2,1,0:T(8,128)S(1)} %get-tuple-element.18.W, ...), custom_call_target="tpu_custom_call" | custom-call | tf_op jit(solution)/shard_map/settle/pallas_call | solution.py:565
